TPU v7x, 32 devices: a whole 2x2x4 slice. The times are simulated.
32 devices in a mesh: grp: 2 (over x), bus: 16 (over z, y, core).
Axes of the slice: x: 2, y: 2, z: 4, core: 2. Of those that a mesh axis runs over, the one named last changes fastest.
Arguments:
- series: bfloat16 [32, 2048, 1024], P(('grp', 'bus')), parts along dimension 0, may hold values from -6 to 6
- hour_ids: int32 [32], P(('grp', 'bus')), parts along dimension 0, may hold values from 0 to 23
- hour_table: bfloat16 [24, 1024], replicated, may hold values from -3 to 3
- norm_gain: float32 [1024], replicated, may hold values from 0.1 to 1.9
- bus_order: int32 [4096], P('grp'), parts along dimension 0, may hold values from 0 to 2047, each once
- w_query: bfloat16 [1024, 512], replicated, may hold values from -0.1875 to 0.1875
- w_key: bfloat16 [1024, 512], replicated, may hold values from -0.1875 to 0.1875
- w_value: bfloat16 [1024, 512], replicated, may hold values from -0.1875 to 0.1875
- score_scale: float32 [8], replicated, may hold values from 0.5 to 10, as said below
- neighbors: int32 [32, 3], P('grp'), parts along dimension 0, may hold values from -1 to 15, as said below
- grad_out: bfloat16 [32, 2048, 512], P('grp', 'bus'), parts along dimension 0, may hold values from -6 to 6
Outputs:
- key_grad: bfloat16 [32, 2048, 512], P('grp', 'bus'), parts along dimension 0
- value_grad: bfloat16 [32, 2048, 512], P('grp', 'bus'), parts along dimension 0
There are 2 independent parts, one for each index of `grp`. A program takes and returns all parts, laid end to end along the dimension named above; an argument that names none is the same for every part. Nothing has to cross between parts.
Inputs may be any that keep to these rules, and one draw needn't show every extreme that they name: `neighbors`: row b lists the key blocks read by query block b: entry 0 is b - 1 or -1, entry 1 is b, entry 2 is b + 1 or -1; -1 marks a block not read, and stands in entry 0 of row 0 and entry 2 of row 15. `score_scale`: positive temperatures of the heads.
All inputs are finite; a program needn't handle non-finite values.
Results may differ from a plain program's by a relative error of at most 0.018.
The roundings to bfloat16 on the way count: a program that leaves them out, or rounds other values in their place, can miss the bound.
Values may be sent and summed in bfloat16 or wider, within the bound.
No kernel may reach another device: no remote copies, remote signals or barrier semaphores. Data moves between devices by JAX's collectives and lax.ppermute only.
A program may use at most 256 MiB of HBM per device.

v0:
```python
import math

import jax
import jax.numpy as jnp
from jax import lax
from jax.sharding import PartitionSpec as P

EPSILON = 1e-05
NEG_FILL = -1e30


def with_halo(shard, sides, width):
    for axis, dim in sides:
        devices, length = (lax.axis_size(axis), shard.shape[dim])
        up = [(i, (i + 1) % devices) for i in range(devices - 1)]
        down = [(j, i) for i, j in up]
        last = lax.slice_in_dim(shard, length - width, length, axis=dim)
        leading = lax.slice_in_dim(shard, 0, width, axis=dim)
        before = lax.ppermute(last, axis, up)
        after = lax.ppermute(leading, axis, down)
        shard = jnp.concatenate([before, shard, after], axis=dim)
    return shard


def from_behind(value, axis, steps):
    count = lax.axis_size(axis)
    leading, last = (max(0, -steps), min(count, count - steps))
    return lax.ppermute(value, axis, [(source, source + steps) for source in range(leading, last)])


def split_heads(array, head_count):
    return array.reshape(array.shape[0], array.shape[1], head_count, array.shape[2] // head_count)


def over_groups(step_fn, arrays, group_size):
    stacked = tuple(
        (
            item.reshape((item.shape[0] // group_size, group_size) + item.shape[1:])
            for item in arrays
        )
    )
    results = lax.map(lambda pieces: step_fn(*pieces), stacked)
    return tuple((item.reshape((-1,) + item.shape[2:]) for item in results))


def reader_terms(queries, key_tiles, value_tiles, grad_rows, colvalid, head_scale):
    scores = (
        jnp.einsum("sihd,sjhd->shij", queries, key_tiles, preferred_element_type=jnp.float32)
        * head_scale[None, :, None, None]
    )
    scores = jnp.where(colvalid[None, None, None, :], scores, NEG_FILL)
    row_max = jnp.max(scores, axis=-1)
    log_total = row_max + jnp.log(jnp.sum(jnp.exp(scores - row_max[..., None]), axis=-1))
    weights = jnp.exp(scores - log_total[..., None])
    weights_b = weights.astype(jnp.bfloat16)
    attended = jnp.einsum(
        "shij,sjhd->sihd", weights_b, value_tiles, preferred_element_type=jnp.float32
    ).astype(jnp.bfloat16)
    row_dot = jnp.einsum("sihd,sihd->shi", grad_rows, attended, preferred_element_type=jnp.float32)
    dweights = jnp.einsum(
        "sihd,sjhd->shij", grad_rows, value_tiles, preferred_element_type=jnp.float32
    )
    dscores = (weights * (dweights - row_dot[..., None]) * head_scale[None, :, None, None]).astype(
        jnp.bfloat16
    )
    value_part = jnp.einsum(
        "shij,sihd->sjhd", weights_b, grad_rows, preferred_element_type=jnp.float32
    )
    key_part = jnp.einsum("shij,sihd->sjhd", dscores, queries, preferred_element_type=jnp.float32)
    return (log_total, row_dot, key_part.astype(jnp.bfloat16), value_part.astype(jnp.bfloat16))


def on_device(
    series,
    hour_ids,
    hour_table,
    norm_gain,
    bus_order,
    w_query,
    w_key,
    w_value,
    score_scale,
    neighbors,
    grad_out,
):
    head_count = score_scale.shape[0]
    snap_count = grad_out.shape[0]
    block_rows = grad_out.shape[1]
    feat_width = grad_out.shape[2]
    head_dim = feat_width // head_count
    ordered = jnp.take(series, bus_order, axis=1)
    onehot = (
        hour_ids[:, None] == jnp.arange(hour_table.shape[0], dtype=jnp.int32)[None, :]
    ).astype(jnp.bfloat16)
    hour_rows = jnp.dot(onehot, hour_table, preferred_element_type=jnp.float32)
    mixed = ordered.astype(jnp.float32) + hour_rows[:, None, :]
    normed = (
        mixed * lax.rsqrt(jnp.mean(mixed * mixed, axis=-1, keepdims=True) + EPSILON) * norm_gain
    ).astype(jnp.bfloat16)
    arrived = lax.all_to_all(normed, "bus", split_axis=1, concat_axis=0, tiled=True)
    flat_rows = arrived.reshape(-1, arrived.shape[2])
    queries, key_rows, value_rows = [
        jnp.dot(flat_rows, weight, preferred_element_type=jnp.float32)
        .astype(jnp.bfloat16)
        .reshape(snap_count, block_rows, feat_width)
        for weight in (w_query, w_key, w_value)
    ]
    dev_index = lax.axis_index("bus")
    own_row = lax.dynamic_slice_in_dim(neighbors, dev_index, 1, 0)[0]
    colvalid = jnp.repeat(own_row >= 0, block_rows)
    head_scale = score_scale / math.sqrt(head_dim)
    group_size = math.gcd(snap_count, max(1, 512 // block_rows))
    kv_tiles = with_halo(jnp.stack([key_rows, value_rows]), (("bus", 2),), block_rows)
    query_heads = split_heads(queries, head_count)
    grad_heads = split_heads(grad_out, head_count)
    key_heads = split_heads(kv_tiles[0], head_count)
    value_heads = split_heads(kv_tiles[1], head_count)

    def full_step(query_part, key_part, value_part, grad_part):
        return reader_terms(query_part, key_part, value_part, grad_part, colvalid, head_scale)

    log_total, row_dot, key_part, value_part = over_groups(
        full_step, (query_heads, key_heads, value_heads, grad_heads), group_size
    )
    partials = jnp.stack(
        [
            key_part.reshape(snap_count, 3 * block_rows, feat_width),
            value_part.reshape(snap_count, 3 * block_rows, feat_width),
        ]
    )
    from_upper = from_behind(partials[:, :, :block_rows], "bus", -1)
    from_lower = from_behind(partials[:, :, 2 * block_rows :], "bus", 1)
    summed = (
        partials[:, :, block_rows : 2 * block_rows].astype(jnp.float32)
        + from_lower.astype(jnp.float32)
        + from_upper.astype(jnp.float32)
    )
    key_grad = summed[0].astype(jnp.bfloat16)
    value_grad = summed[1].astype(jnp.bfloat16)
    return (key_grad, value_grad)


def solution(mesh):
    return jax.shard_map(
        on_device,
        mesh=mesh,
        in_specs=(
            P(("grp", "bus"), None, None),
            P(("grp", "bus")),
            P(),
            P(),
            P("grp"),
            P(),
            P(),
            P(),
            P(),
            P("grp", None),
            P("grp", "bus", None),
        ),
        out_specs=(P("grp", "bus", None), P("grp", "bus", None)),
        check_vma=False,
    )
```

profile of v0, /device:TPU:12, one launch (start us, length us, event | category | flops | bytes accessed | tf_op | source)
XLA Modules:
  0.0 511.9 jit_solution(18104541909109588138)
XLA Ops:
  2.8 13.7 %gather_fusion = bf16[2048,1024]{1,0:T(8,128)(2,1)} fusion(bf16[2048,1024]{1,0:T(8,128)(2,1)} %bitcast.128, s32[2048]{0:T(1024)S(1)} %fusion.71), kind=kCustom, calls=%fused_computation | custom fusion | bytes 8396800 | tf_op jit(solution)/shard_map/jit(_take)/gather | solution.py:91
  16.6 3.6 multiply_reduce_fusion
  22.0 28.7 %copy.65 = bf16[1,2048,1024]{2,0,1:T(2,128)(2,1)} copy(bf16[1,2048,1024]{2,1,0:T(8,128)(2,1)S(1)} %multiply_convert_fusion.6) | data formatting | bytes 8388608 | tf_op jit(solution)/shard_map/convert_element_type | solution.py:99
  51.3 25.9 %reduce.5 = bf16[2048,1024]{1,0:T(8,128)(2,1)} reduce(bf16[2048,1,1024]{2,1,0:T(2,128)(2,1)} %bitcast.129, bf16[]{:T(256)} %broadcast.169), dimensions={1}, to_apply=%bitcast.102.reduce_sub_computation | reduce | bytes 8388610
  77.2 11.4 %reshape.223 = bf16[16,2,65536]{2,1,0:T(2,128)(2,1)} reshape(bf16[2048,1024]{1,0:T(8,128)(2,1)} %reduce.5) | data formatting | bytes 8388608
  88.6 98.4 %all_to_all.4 = bf16[16,2,65536]{2,1,0:T(2,128)(2,1)} all-to-all(bf16[16,2,65536]{2,1,0:T(2,128)(2,1)} %reshape.223), channel_id=1, replica_groups=mesh['grp'=2,'bus'=16] {'bus'}, dimensions={0} | all-to-all | bytes 8388608 | tf_op jit(solution)/shard_map/all_to_all | solution.py:100
  187.0 12.3 %reshape.224 = bf16[2048,1,1024]{2,1,0:T(2,128)(2,1)} reshape(bf16[16,2,65536]{2,1,0:T(2,128)(2,1)} %all_to_all.4) | data formatting | bytes 8388608
  199.3 7.1 %fusion.65 = bf16[2048,512]{1,0:T(8,128)(2,1)} fusion(bf16[1024,512]{1,0:T(8,128)(2,1)S(1)} %copy-done, bf16[1,2048,1024]{2,0,1:T(2,128)(2,1)} %bitcast.135), kind=kOutput, calls=%fused_computation.64 | convolution fusion | flops 2148532224 | bytes 7340032 | tf_op jit(solution)/shard_map/dot_general | solution.py:103
  206.4 3.0 copy.36
  209.5 7.3 %fusion.68 = bf16[2048,512]{1,0:T(8,128)(2,1)} fusion(bf16[1024,512]{1,0:T(8,128)(2,1)} %param.20, bf16[1,2048,1024]{2,0,1:T(2,128)(2,1)} %bitcast.136), kind=kOutput, calls=%fused_computation.65 | convolution fusion | flops 2148532224 | bytes 7340032 | tf_op jit(solution)/shard_map/dot_general | solution.py:103
  216.8 3.9 copy.37
  220.7 3.9 pad_maximum_fusion.2
  224.7 2.2 collective-permute-start
  226.9 3.6 collective-permute-start.1
  230.5 3.9 copy.38
  234.6 7.3 %fusion.62 = bf16[2048,512]{1,0:T(8,128)(2,1)} fusion(bf16[1024,512]{1,0:T(8,128)(2,1)} %param.18, bf16[1,2048,1024]{2,0,1:T(2,128)(2,1)} %bitcast.137), kind=kOutput, calls=%fused_computation.63 | convolution fusion | flops 2148532224 | bytes 7340032 | tf_op jit(solution)/shard_map/dot_general | solution.py:103
  241.9 6.1 %reshape.221 = bf16[4,4,128,8,64]{4,3,2,1,0:T(8,128)(2,1)} reshape(bf16[2048,512]{1,0:T(8,128)(2,1)} %fusion.62) | data formatting | bytes 4194304 | tf_op jit(solution)/shard_map/reshape;reshape;reshape | solution.py:38
  248.1 5.1 copy.39
  253.1 66.6 %collective-permute-done = bf16[2,16,128,512]{2,3,1,0:T(8,128)(2,1)} collective-permute-done((bf16[2,16,128,512]{2,3,1,0:T(8,128)(2,1)}, bf16[2,16,128,512]{2,3,1,0:T(8,128)(2,1)}, u32[]{:S(2)}, u32[]{:S(2)}) %collective-permute-start) | collective-permute-done | bytes 4194336 | tf_op jit(solution)/shard_map/ppermute | solution.py:19
  319.7 6.3 %pad_maximum_fusion = bf16[2,16,384,512]{2,3,1,0:T(8,128)(2,1)S(1)} fusion(bf16[2,16,128,512]{2,3,1,0:T(8,128)(2,1)} %collective-permute-done.1, bf16[1,16,128,512]{2,3,1,0:T(8,128)(2,1)} %copy.37, bf16[1,16,128,512]{2,3,1,0:T(8,128)(2,1)S(1)} %copy.36, bf16[2,16,128,512]{2,3,1,0:T(8,128)(2,1)} %collective-permute-done), kind=kLoop, calls=%fused_computation.47 | loop fusion | flops 50331648 | bytes 25165824 | tf_op jit(solution)/shard_map/concatenate | solution.py:21
  326.1 5.9 %fusion.81 = (bf16[1,16,384,512]{2,3,1,0:T(8,128)(2,1)}, bf16[1,16,384,512]{2,3,1,0:T(8,128)(2,1)}) fusion(bf16[2,16,384,512]{2,3,1,0:T(8,128)(2,1)S(1)} %pad_maximum_fusion), kind=kLoop, calls=%fused_computation.83 | loop fusion | bytes 25165824 | tf_op jit(solution)/shard_map/slice | solution.py:117
  332.0 70.7 %while.13 = (s32[]{:T(128)}, bf16[4,4,384,8,64]{2,4,3,1,0:T(8,128)(2,1)}, bf16[4,4,384,8,64]{2,4,3,1,0:T(8,128)(2,1)}, bf16[4,4,128,8,64]{2,4,3,1,0:T(8,128)(2,1...) while((s32[]{:T(128)}, ...), condition=%wide.region_4.5_spmd.clone, body=%wide.region_1.0_spmd.clone.sunk | while | flops 1044111360 | bytes 75687264 | solution.py:42
  332.1 2.8 fusion.102
  334.9 2.3 exponential_reduce_fusion.2
  337.2 2.8 bitcast_dynamic-update-slice_fusion.5
  340.1 3.4 fusion.103
  343.5 6.2 %bitcast_dynamic-update-slice_fusion.4 = bf16[4,4,384,8,64]{2,4,3,1,0:T(8,128)(2,1)} fusion(bf16[4,4,384,8,64]{2,4,3,1,0:T(8,128)(2,1)} %get-tuple-element.211, s32[]{:T(128)} %get-tuple-element.210, f32[4,8,128,384]{3,2,1,0:T(8,128)} %copy-done.2, f32[4,8,128]{2,1,0:T(8,128)S(1)} %fusion.103, f32[4,8,128]{2,1,0:T(8,128)S(1)} %log_add_fusion.2, ...), kind=kOutput, calls=%fused_computation.14.clone.1 | convolution fusion | flops 414449664 | bytes 10521600 | tf_op jit(solution)/shard_map/while/body/eval_jaxpr/shij,sihd->sjhd/dot_general | solution.py:69
  349.7 2.8 fusion.102
  352.5 2.3 exponential_reduce_fusion.2
  354.9 2.8 bitcast_dynamic-update-slice_fusion.5
  357.7 3.4 fusion.103
  361.2 6.2 %bitcast_dynamic-update-slice_fusion.4 = bf16[4,4,384,8,64]{2,4,3,1,0:T(8,128)(2,1)} fusion(bf16[4,4,384,8,64]{2,4,3,1,0:T(8,128)(2,1)} %get-tuple-element.211, s32[]{:T(128)} %get-tuple-element.210, f32[4,8,128,384]{3,2,1,0:T(8,128)} %copy-done.2, f32[4,8,128]{2,1,0:T(8,128)S(1)} %fusion.103, f32[4,8,128]{2,1,0:T(8,128)S(1)} %log_add_fusion.2, ...), kind=kOutput, calls=%fused_computation.14.clone.1 | convolution fusion | flops 414449664 | bytes 10521600 | tf_op jit(solution)/shard_map/while/body/eval_jaxpr/shij,sihd->sjhd/dot_general | solution.py:69
  367.4 2.8 fusion.102
  370.2 2.3 exponential_reduce_fusion.2
  372.6 2.9 bitcast_dynamic-update-slice_fusion.5
  375.5 3.4 fusion.103
  378.9 6.2 %bitcast_dynamic-update-slice_fusion.4 = bf16[4,4,384,8,64]{2,4,3,1,0:T(8,128)(2,1)} fusion(bf16[4,4,384,8,64]{2,4,3,1,0:T(8,128)(2,1)} %get-tuple-element.211, s32[]{:T(128)} %get-tuple-element.210, f32[4,8,128,384]{3,2,1,0:T(8,128)} %copy-done.2, f32[4,8,128]{2,1,0:T(8,128)S(1)} %fusion.103, f32[4,8,128]{2,1,0:T(8,128)S(1)} %log_add_fusion.2, ...), kind=kOutput, calls=%fused_computation.14.clone.1 | convolution fusion | flops 414449664 | bytes 10521600 | tf_op jit(solution)/shard_map/while/body/eval_jaxpr/shij,sihd->sjhd/dot_general | solution.py:69
  385.1 2.8 fusion.102
  387.9 2.3 exponential_reduce_fusion.2
  390.3 2.8 bitcast_dynamic-update-slice_fusion.5
  393.1 3.4 fusion.103
  396.6 6.2 %bitcast_dynamic-update-slice_fusion.4 = bf16[4,4,384,8,64]{2,4,3,1,0:T(8,128)(2,1)} fusion(bf16[4,4,384,8,64]{2,4,3,1,0:T(8,128)(2,1)} %get-tuple-element.211, s32[]{:T(128)} %get-tuple-element.210, f32[4,8,128,384]{3,2,1,0:T(8,128)} %copy-done.2, f32[4,8,128]{2,1,0:T(8,128)S(1)} %fusion.103, f32[4,8,128]{2,1,0:T(8,128)S(1)} %log_add_fusion.2, ...), kind=kOutput, calls=%fused_computation.14.clone.1 | convolution fusion | flops 414449664 | bytes 10521600 | tf_op jit(solution)/shard_map/while/body/eval_jaxpr/shij,sihd->sjhd/dot_general | solution.py:69
  402.7 4.0 fusion.54
  406.7 2.6 collective-permute-start.2
  409.3 3.5 collective-permute-start.3
  412.8 88.9 %collective-permute-done.2 = bf16[2,16,128,512]{2,3,1,0:T(8,128)(2,1)S(1)} collective-permute-done((bf16[2,16,128,512]{2,3,1,0:T(8,128)(2,1)S(1)}, bf16[2,16,128,512]{2,3,1,0:T(8,128)(2,1)S(1)}, u32[]{:S(2)}, u32[]{:S(2)}) %collective-permute-start.2) | collective-permute-done | bytes 4194336 | tf_op jit(solution)/shard_map/ppermute | solution.py:28
  505.4 3.9 copy.40
  509.3 2.6 copy.41
  (58 shorter events, 8.1 us)
Async XLA Ops:
  0.6 198.7 %copy-start = (bf16[1024,512]{1,0:T(8,128)(2,1)S(1)}, bf16[1024,512]{1,0:T(8,128)(2,1)}, u32[]{:S(2)}) copy-start(bf16[1024,512]{1,0:T(8,128)(2,1)} %param.19) | copy-start | bytes 3145732
  2.8 13.7 %copy-start.8 = (bf16[24,1024]{1,0:T(8,128)(2,1)S(1)}, bf16[24,1024]{1,0:T(8,128)(2,1)}, u32[]{:S(2)}) copy-start(bf16[24,1024]{1,0:T(8,128)(2,1)} %param.15) | copy-start | bytes 147460
  2.8 17.5 %copy-start.9 = (f32[1024]{0:T(1024)S(1)}, f32[1024]{0:T(1024)}, u32[]{:S(2)}) copy-start(f32[1024]{0:T(1024)} %param.16) | copy-start | bytes 12292
  16.5 3.8 copy-start.3
  220.7 13.7 %copy-start.10 = (s32[16,3]{0,1:T(4,128)S(1)}, s32[16,3]{0,1:T(4,128)}, u32[]{:S(2)}) copy-start(s32[16,3]{0,1:T(4,128)} %param.22) | copy-start | bytes 580
  220.7 13.9 %copy-start.11 = (f32[8]{0:T(128)S(1)}, f32[8]{0:T(128)}, u32[]{:S(2)}) copy-start(f32[8]{0:T(128)} %param.21) | copy-start | bytes 100
  224.7 95.1 %collective-permute-start = (bf16[2,16,128,512]{2,3,1,0:T(8,128)(2,1)}, bf16[2,16,128,512]{2,3,1,0:T(8,128)(2,1)}, u32[]{:S(2)}, u32[]{:S(2)}) collective-permute-start(bf16[2,16,128,512]{2,3,1,0:T(8,128)(2,1)} %pad_maximum_fusion.2), channel_id=1, source_target_pairs={{0,1},{1,2},{2,3},{3,4},{4,5},{5,6},{6,7},{7,8},{8,9},{9,10},{10,1... | collective-permute-start | bytes 12582920 | tf_op jit(solution)/shard_map/ppermute | solution.py:19
  226.9 92.9 %collective-permute-start.1 = (bf16[2,16,128,512]{2,3,1,0:T(8,128)(2,1)}, bf16[2,16,128,512]{2,3,1,0:T(8,128)(2,1)}, u32[]{:S(2)}, u32[]{:S(2)}) collective-permute-start(bf16[2,16,128,512]{2,3,1,0:T(8,128)(2,1)} %pad_maximum_fusion.2), channel_id=1, source_target_pairs={{1,0},{2,1},{3,2},{4,3},{5,4},{6,5},{7,6},{8,7},{9,8},{10,9},{11,1... | collective-permute-start | bytes 12582920 | tf_op jit(solution)/shard_map/ppermute | solution.py:20
  326.1 6.0 %copy-start.6 = (bf16[4,4,128,8,64]{2,4,3,1,0:T(8,128)(2,1)S(1)}, bf16[4,4,128,8,64]{2,4,3,1,0:T(8,128)(2,1)}, u32[]{:S(2)}) copy-start(bf16[4,4,128,8,64]{2,4,3,1,0:T(8,128)(2,1)} %copy.39) | copy-start | bytes 6291460
  332.1 5.1 %copy-start.7 = (bf16[4,4,128,8,64]{2,4,3,1,0:T(8,128)(2,1)S(1)}, bf16[4,4,128,8,64]{2,4,3,1,0:T(8,128)(2,1)}, u32[]{:S(2)}) copy-start(bf16[4,4,128,8,64]{2,4,3,1,0:T(8,128)(2,1)} %get-tuple-element.226) | copy-start | bytes 6291460 | tf_op jit(solution)/shard_map/while
  334.9 5.2 %copy-start.2 = (f32[4,8,128,384]{3,2,1,0:T(8,128)}, f32[4,8,128,384]{3,2,1,0:T(8,128)S(1)}, u32[]{:S(2)}) copy-start(f32[4,8,128,384]{3,2,1,0:T(8,128)S(1)} %get-tuple-element.198) | copy-start | bytes 18874372 | tf_op jit(solution)/shard_map/while
  349.7 5.1 %copy-start.7 = (bf16[4,4,128,8,64]{2,4,3,1,0:T(8,128)(2,1)S(1)}, bf16[4,4,128,8,64]{2,4,3,1,0:T(8,128)(2,1)}, u32[]{:S(2)}) copy-start(bf16[4,4,128,8,64]{2,4,3,1,0:T(8,128)(2,1)} %get-tuple-element.226) | copy-start | bytes 6291460 | tf_op jit(solution)/shard_map/while
  352.5 5.2 %copy-start.2 = (f32[4,8,128,384]{3,2,1,0:T(8,128)}, f32[4,8,128,384]{3,2,1,0:T(8,128)S(1)}, u32[]{:S(2)}) copy-start(f32[4,8,128,384]{3,2,1,0:T(8,128)S(1)} %get-tuple-element.198) | copy-start | bytes 18874372 | tf_op jit(solution)/shard_map/while
  367.4 5.1 %copy-start.7 = (bf16[4,4,128,8,64]{2,4,3,1,0:T(8,128)(2,1)S(1)}, bf16[4,4,128,8,64]{2,4,3,1,0:T(8,128)(2,1)}, u32[]{:S(2)}) copy-start(bf16[4,4,128,8,64]{2,4,3,1,0:T(8,128)(2,1)} %get-tuple-element.226) | copy-start | bytes 6291460 | tf_op jit(solution)/shard_map/while
  370.2 5.2 %copy-start.2 = (f32[4,8,128,384]{3,2,1,0:T(8,128)}, f32[4,8,128,384]{3,2,1,0:T(8,128)S(1)}, u32[]{:S(2)}) copy-start(f32[4,8,128,384]{3,2,1,0:T(8,128)S(1)} %get-tuple-element.198) | copy-start | bytes 18874372 | tf_op jit(solution)/shard_map/while
  385.1 5.1 %copy-start.7 = (bf16[4,4,128,8,64]{2,4,3,1,0:T(8,128)(2,1)S(1)}, bf16[4,4,128,8,64]{2,4,3,1,0:T(8,128)(2,1)}, u32[]{:S(2)}) copy-start(bf16[4,4,128,8,64]{2,4,3,1,0:T(8,128)(2,1)} %get-tuple-element.226) | copy-start | bytes 6291460 | tf_op jit(solution)/shard_map/while
  387.9 5.2 %copy-start.2 = (f32[4,8,128,384]{3,2,1,0:T(8,128)}, f32[4,8,128,384]{3,2,1,0:T(8,128)S(1)}, u32[]{:S(2)}) copy-start(f32[4,8,128,384]{3,2,1,0:T(8,128)S(1)} %get-tuple-element.198) | copy-start | bytes 18874372 | tf_op jit(solution)/shard_map/while
  402.7 99.0 %copy-start.4 = (bf16[4,4,384,8,64]{2,4,3,1,0:T(8,128)(2,1)S(1)}, bf16[4,4,384,8,64]{2,4,3,1,0:T(8,128)(2,1)}, u32[]{:S(2)}) copy-start(bf16[4,4,384,8,64]{2,4,3,1,0:T(8,128)(2,1)} %get-tuple-element.50) | copy-start | bytes 18874372
  402.7 99.0 %copy-start.5 = (bf16[4,4,384,8,64]{2,4,3,1,0:T(8,128)(2,1)S(1)}, bf16[4,4,384,8,64]{2,4,3,1,0:T(8,128)(2,1)}, u32[]{:S(2)}) copy-start(bf16[4,4,384,8,64]{2,4,3,1,0:T(8,128)(2,1)} %get-tuple-element.51) | copy-start | bytes 18874372
  406.7 95.0 %collective-permute-start.2 = (bf16[2,16,128,512]{2,3,1,0:T(8,128)(2,1)S(1)}, bf16[2,16,128,512]{2,3,1,0:T(8,128)(2,1)S(1)}, u32[]{:S(2)}, u32[]{:S(2)}) collective-permute-start(bf16[2,16,128,512]{2,3,1,0:T(8,128)(2,1)S(1)} %get-tuple-element.135), channel_id=1, source_target_pairs={{0,1},{1,2},{2,3},{3,4},{4,5},{5,6},{6,7},{7,8},{8,9},{9,10},{10,1... | collective-permute-start | bytes 12582920 | tf_op jit(solution)/shard_map/ppermute | solution.py:28
  409.3 92.4 %collective-permute-start.3 = (bf16[2,16,128,512]{2,3,1,0:T(8,128)(2,1)S(1)}, bf16[2,16,128,512]{2,3,1,0:T(8,128)(2,1)S(1)}, u32[]{:S(2)}, u32[]{:S(2)}) collective-permute-start(bf16[2,16,128,512]{2,3,1,0:T(8,128)(2,1)S(1)} %get-tuple-element.136), channel_id=1, source_target_pairs={{1,0},{2,1},{3,2},{4,3},{5,4},{6,5},{7,6},{8,7},{9,8},{10,9},{11,1... | collective-permute-start | bytes 12582920 | tf_op jit(solution)/shard_map/ppermute | solution.py:28
  503.7 8.2 %copy-start.1 = (bf16[1024,512]{1,0:T(8,128)(2,1)S(1)}, bf16[1024,512]{1,0:T(8,128)(2,1)}, u32[]{:S(2)}) copy-start(bf16[1024,512]{1,0:T(8,128)(2,1)} %param.19) | copy-start | bytes 3145732
where the time goes:
time: 513 us; the launch traced here: 512 us
  waiting for transfers between devices  156 us (30%)
  local copies, waits for them, and re-layouts  103 us (20%)
  blocking collectives  98.4 us (19%)
  matrix products  82.8 us (16%)
  other arithmetic  58.4 us (11%)
  starting transfers between devices  11.9 us (2%)
    all_to_all x1, blocking collectives, on_device(): lax.all_to_all(normed, 'bus', split_axis=1, concat_axis=0, tiled=True)  98.4 us
    ppermute x2, waiting for transfers between devices, from_behind(): lax.ppermute(value, axis, [(source, source + steps) for source in range(l...  88.9 us
    ppermute x1, waiting for transfers between devices, with_halo(): before = lax.ppermute(last, axis, up)  66.6 us
    unnamed x27, local copies, waits for them, and re-layouts  39.7 us
    convert_element_type x1, local copies, waits for them, and re-layouts, on_device(): normed = (mixed * lax.rsqrt(jnp.mean(mixed * mixed, axis=-1, keepdims=Tru...  28.7 us
    unnamed x1, other arithmetic  25.9 us
    dot_general x4, matrix products, reader_terms(): jnp.einsum('shij,sihd->sjhd', dscores, queries, preferred_element_type=jn...  24.6 us
    dot_general x3, matrix products, on_device(): jnp.dot(flat_rows, weight, preferred_element_type=jnp.float32)  21.8 us
  transfers between devices with their start and end apart: 4, of which 2 were waited for; matrix products, arithmetic and copies ran while one was open for 4% of the time, Pallas kernels for 0%

commit v1 on v0

v1 whole, which is shorter than its diff:
```python
import functools
import math

import jax
import jax.numpy as jnp
from jax import lax
from jax.experimental import pallas as pl
from jax.experimental.pallas import tpu as pltpu
from jax.sharding import PartitionSpec as P

EPSILON = 1e-05
NEG_FILL = -1e30


def nt_dot(a, b):
    return lax.dot_general(a, b, (((1,), (1,)), ((), ())), preferred_element_type=jnp.float32)


def tn_dot(a, b):
    return lax.dot_general(a, b, (((0,), (0,)), ((), ())), preferred_element_type=jnp.float32)


def encode_kernel(
    hour_ref, order_ref, series_ref, table_ref, gain_ref, wq_ref, wk_ref, wv_ref, q_ref, k_ref, v_ref
):
    tile = order_ref.shape[0]
    buses = series_ref.shape[0]
    hours = table_ref.shape[0]
    pick = lax.broadcasted_iota(jnp.int32, (tile, buses), 1) == order_ref[...]
    ordered = jnp.dot(
        pick.astype(jnp.bfloat16), series_ref[...], preferred_element_type=jnp.float32
    )
    table = table_ref[...].astype(jnp.float32)
    is_hour = lax.broadcasted_iota(jnp.int32, (hours, 1), 0) == hour_ref[0]
    hour_row = jnp.sum(jnp.where(is_hour, table, 0.0), axis=0, keepdims=True)
    mixed = ordered + hour_row
    power = jnp.mean(mixed * mixed, axis=1, keepdims=True)
    normed = (mixed * lax.rsqrt(power + EPSILON) * gain_ref[...]).astype(jnp.bfloat16)
    for weight_ref, out_ref in ((wq_ref, q_ref), (wk_ref, k_ref), (wv_ref, v_ref)):
        out_ref[...] = jnp.dot(
            normed, weight_ref[...], preferred_element_type=jnp.float32
        ).astype(jnp.bfloat16)


def encode(series, hour_ids, hour_table, norm_gain, order, w_query, w_key, w_value, tile):
    buses, width = series.shape
    feat = w_query.shape[1]
    whole = lambda shape: pl.BlockSpec(shape, lambda i, *_: (0, 0))
    row_spec = pl.BlockSpec((tile, feat), lambda i, *_: (i, 0))
    out = jax.ShapeDtypeStruct((buses, feat), jnp.bfloat16)
    return pl.pallas_call(
        encode_kernel,
        grid_spec=pltpu.PrefetchScalarGridSpec(
            num_scalar_prefetch=1,
            grid=(buses // tile,),
            in_specs=[
                pl.BlockSpec((tile, 1), lambda i, *_: (i, 0)),
                whole((buses, width)),
                whole(hour_table.shape),
                whole((1, width)),
                whole((width, feat)),
                whole((width, feat)),
                whole((width, feat)),
            ],
            out_specs=[row_spec, row_spec, row_spec],
        ),
        out_shape=[out, out, out],
        compiler_params=pltpu.CompilerParams(vmem_limit_bytes=48 << 20),
        cost_estimate=pl.CostEstimate(
            flops=2 * buses * width * (buses + 3 * feat),
            bytes_accessed=2 * (buses * width + 3 * width * feat + 3 * buses * feat),
            transcendentals=buses,
        ),
        name="encode",
    )(
        hour_ids,
        order.reshape(buses, 1),
        series,
        hour_table,
        norm_gain.reshape(1, width),
        w_query,
        w_key,
        w_value,
    )


def attend_kernel(
    rows, neighbors_ref, scale_ref, q_ref, k_ref, v_ref, g_ref, dk_ref, dv_ref, k_acc, v_acc
):
    pair = pl.program_id(0)
    blocks = q_ref.shape[0] // rows
    lanes = q_ref.shape[1]
    half = lanes // 2
    first_half = lax.broadcasted_iota(jnp.int32, (rows, lanes), 1) < half
    zero = jnp.zeros((rows, lanes), jnp.bfloat16)
    col = lax.broadcasted_iota(jnp.int32, (1, 2 * rows), 1)
    scale = jnp.where(col < rows, scale_ref[2 * pair], scale_ref[2 * pair + 1])
    k_acc[...] = jnp.zeros_like(k_acc)
    v_acc[...] = jnp.zeros_like(v_acc)

    def both_heads(x):
        return jnp.concatenate([jnp.where(first_half, x, zero), jnp.where(first_half, zero, x)], 0)

    def step(b, carry):
        def tile_at(ref, block):
            return ref[pl.ds(pl.multiple_of(block * rows, rows), rows), :]

        near = [jnp.maximum(b - 1, 0), b, jnp.minimum(b + 1, blocks - 1)]
        q_two = both_heads(tile_at(q_ref, b))
        g_own = tile_at(g_ref, b)
        g_two = both_heads(g_own)
        keys = jnp.concatenate([tile_at(k_ref, c) for c in near], 0)
        values = jnp.concatenate([tile_at(v_ref, c) for c in near], 0)
        raw = nt_dot(keys, q_two)
        scores = jnp.concatenate(
            [
                jnp.where(
                    neighbors_ref[b, d] >= 0, raw[d * rows : (d + 1) * rows] * scale, NEG_FILL
                )
                for d in range(3)
            ],
            0,
        )
        row_max = jnp.max(scores, axis=0, keepdims=True)
        powers = jnp.exp(scores - row_max)
        total = jnp.sum(powers, axis=0, keepdims=True)
        weights = powers * (1.0 / total)
        weights_b = weights.astype(jnp.bfloat16)
        attended = tn_dot(values, weights_b).astype(jnp.bfloat16).astype(jnp.float32)
        g_turned = g_own.astype(jnp.float32).T
        row_dot = jnp.concatenate(
            [
                jnp.sum(g_turned[:half] * attended[:half, :rows], axis=0, keepdims=True),
                jnp.sum(g_turned[half:] * attended[half:, rows:], axis=0, keepdims=True),
            ],
            1,
        )
        dweights = nt_dot(values, g_two)
        dscores = (weights * (dweights - row_dot) * scale).astype(jnp.bfloat16)
        v_part = jnp.dot(weights_b, g_two, preferred_element_type=jnp.float32)
        k_part = jnp.dot(dscores, q_two, preferred_element_type=jnp.float32)
        at = pl.ds(pl.multiple_of(b * rows, rows), 3 * rows)
        k_acc[at, :] += k_part
        v_acc[at, :] += v_part
        return carry

    lax.fori_loop(0, blocks, step, 0, unroll=2)
    inner = pl.ds(rows, blocks * rows)
    dk_ref[...] = k_acc[inner, :].astype(jnp.bfloat16)
    dv_ref[...] = v_acc[inner, :].astype(jnp.bfloat16)


def attend(queries, keys, values, grads, neighbors, head_scale, rows):
    buses, feat = queries.shape
    heads = head_scale.shape[0]
    lanes = 2 * feat // heads
    spec = pl.BlockSpec((buses, lanes), lambda p, *_: (0, p))
    out = jax.ShapeDtypeStruct((buses, feat), jnp.bfloat16)
    return pl.pallas_call(
        functools.partial(attend_kernel, rows),
        grid_spec=pltpu.PrefetchScalarGridSpec(
            num_scalar_prefetch=2,
            grid=(heads // 2,),
            in_specs=[spec] * 4,
            out_specs=[spec, spec],
            scratch_shapes=[
                pltpu.VMEM((buses + 2 * rows, lanes), jnp.float32),
                pltpu.VMEM((buses + 2 * rows, lanes), jnp.float32),
            ],
        ),
        out_shape=[out, out],
        compiler_params=pltpu.CompilerParams(vmem_limit_bytes=48 << 20),
        cost_estimate=pl.CostEstimate(
            flops=2 * 5 * 3 * rows * buses * feat,
            bytes_accessed=2 * 6 * buses * feat,
            transcendentals=3 * rows * buses * heads,
        ),
        name="attend",
    )(neighbors, head_scale, queries, keys, values, grads)


def on_device(
    series,
    hour_ids,
    hour_table,
    norm_gain,
    bus_order,
    w_query,
    w_key,
    w_value,
    score_scale,
    neighbors,
    grad_out,
):
    head_count = score_scale.shape[0]
    snap_count, block_rows, feat_width = grad_out.shape
    own_snaps, bus_count, _ = series.shape
    devices = lax.axis_size("bus")
    head_scale = score_scale / math.sqrt(feat_width // head_count)
    grads = lax.all_to_all(grad_out, "bus", split_axis=0, concat_axis=1, tiled=True)
    results = []
    for s in range(own_snaps):
        queries, keys, values = encode(
            series[s], hour_ids[s : s + 1], hour_table, norm_gain, bus_order,
            w_query, w_key, w_value, math.gcd(bus_count, 256),
        )
        results.append(
            attend(queries, keys, values, grads[s], neighbors, head_scale, block_rows)
        )
    both = jnp.stack([jnp.stack(pieces) for pieces in zip(*results)])
    both = both.reshape(2, own_snaps, devices, block_rows, feat_width).transpose(2, 0, 1, 3, 4)
    back = lax.all_to_all(both, "bus", split_axis=0, concat_axis=0, tiled=True)
    back = back.transpose(1, 0, 2, 3, 4).reshape(2, snap_count, block_rows, feat_width)
    return (back[0], back[1])


def solution(mesh):
    return jax.shard_map(
        on_device,
        mesh=mesh,
        in_specs=(
            P(("grp", "bus"), None, None),
            P(("grp", "bus")),
            P(),
            P(),
            P("grp"),
            P(),
            P(),
            P(),
            P(),
            P("grp", None),
            P("grp", "bus", None),
        ),
        out_specs=(P("grp", "bus", None), P("grp", "bus", None)),
        check_vma=False,
    )
```

time: 513 us -> 201 us (0.39)
  waiting for transfers between devices: 156 us -> 23.8 us
  local copies, waits for them, and re-layouts: 103 us -> 3.98 us
  matrix products: 82.8 us -> 0 us
  Pallas kernels: 0 us -> 66.4 us
  other arithmetic: 58.4 us -> 0.39 us
  starting transfers between devices: 11.9 us -> 6.38 us
    ppermute x4 -> x0, waiting for transfers between devices: 156 us -> none  [the longest x2 88.9 us: from_behind(): lax.ppermute(value, axis, [(source, source + steps) for source in range(l...]
    dot_general x20 -> x0, matrix products: 82.8 us -> none  [the longest x4 24.6 us: reader_terms(): jnp.einsum('shij,sihd->sjhd', dscores, queries, preferred_element_type=jn...]
    pallas_call x0 -> x2, Pallas kernels: none -> 66.4 us  [the longest x1 45.3 us: attend(): pl.pallas_call(functools.partial(attend_kernel, rows), grid_spec=pltpu.Pr...]
    unnamed x27 -> x17, local copies, waits for them, and re-layouts: 39.7 us -> 1.33 us
    convert_element_type x2 -> x0, local copies, waits for them, and re-layouts: 30.4 us -> none  [the longest x1 28.7 us: on_device(): normed = (mixed * lax.rsqrt(jnp.mean(mixed * mixed, axis=-1, keepdims=Tru...]
    unnamed x1 -> x0, other arithmetic: 25.9 us -> none
    all_to_all x0 -> x1, waiting for transfers between devices: none -> 23.8 us  [on_device(): lax.all_to_all(grad_out, 'bus', split_axis=0, concat_axis=1, tiled=True)]
    gather x1 -> x0, local copies, waits for them, and re-layouts: 13.7 us -> none  [on_device(): ordered = jnp.take(series, bus_order, axis=1)]
  transfers between devices with their start and end apart: 4 -> 1, of which waited for: 2 -> 1; matrix products, arithmetic and copies ran while one was open for 4% -> 0% of each run, Pallas kernels for 0% -> 11%
where the time goes in v1:
time: 201 us; the launch traced here: 199 us
  blocking collectives  97 us (48%)
  Pallas kernels  66.4 us (33%)
  waiting for transfers between devices  23.8 us (12%)
  starting transfers between devices  6.38 us (3%)
  local copies, waits for them, and re-layouts  3.98 us (2%)
    all_to_all x1, blocking collectives, on_device(): back = lax.all_to_all(both, 'bus', split_axis=0, concat_axis=0, tiled=True)  97 us
    pallas_call x1, Pallas kernels, attend(): pl.pallas_call(functools.partial(attend_kernel, rows), grid_spec=pltpu.Pr...  45.3 us
    all_to_all x1, waiting for transfers between devices, on_device(): lax.all_to_all(grad_out, 'bus', split_axis=0, concat_axis=1, tiled=True)  23.8 us
    pallas_call x1, Pallas kernels, encode(): pl.pallas_call(encode_kernel, grid_spec=pltpu.PrefetchScalarGridSpec(num_...  21.1 us
    all_to_all x1, starting transfers between devices, on_device(): lax.all_to_all(grad_out, 'bus', split_axis=0, concat_axis=1, tiled=True)  6.38 us
  transfers between devices with their start and end apart: 1, of which 1 were waited for; matrix products, arithmetic and copies ran while one was open for 0% of the time, Pallas kernels for 11%

profile of v1, /device:TPU:12, one launch (start us, length us, event | category | flops | bytes accessed | tf_op | source)
XLA Modules:
  0.0 199.4 jit_solution(10886798443855822522)
XLA Ops:
  0.6 0.0 copy-start.6
  0.6 0.0 copy-start.5
  0.7 0.0 copy-start.7
  0.7 0.0 copy-start.1
  0.7 0.0 copy-start
  0.7 0.0 copy-start.4
  0.7 0.0 copy-start.3
  0.7 6.4 %all-to-all-start = ((bf16[16,128,512]{2,1,0:T(8,128)(2,1)}), bf16[16,128,512]{2,1,0:T(8,128)(2,1)}, u32[]{:S(2)}, u32[]{:S(2)}) async-start(bf16[16,128,512]{2,1,0:T(8,128)(2,1)} %param.21), calls=%async_computation | async-start | bytes 4194304 | tf_op jit(solution)/shard_map/all_to_all | solution.py:200
  7.7 0.0 copy-done.6
  7.7 0.1 copy.17.neighbors_ref
  7.8 0.0 copy-done.5
  7.8 0.4 copy.16.order_ref
  8.2 0.0 copy-done.7
  8.2 0.0 copy-done.1
  8.2 0.0 copy-done
  8.2 0.0 copy-done.4
  8.3 0.0 copy-done.3
  8.3 0.0 copy-start.2
  8.3 1.2 copy-done.2
  9.5 21.1 %encode.1 = (bf16[2048,512]{1,0:T(8,128)(2,1)}, bf16[2048,512]{1,0:T(8,128)(2,1)}, bf16[2048,512]{1,0:T(8,128)(2,1)}) custom-call(s32[1]{0:T(128)S(6)} %copy.20.hour_ref, s32[2048,1]{1,0:T(8,128)S(1)} %copy.16.order_ref, bf16[2048,1024]{1,0:T(8,128)(2,1)} %bitcast.22, bf16[24,1024]{1,0:T(8,128)(2,1)S(1)} %copy-done.3, f32[1,1024]{1,0:T(1,128)S(1)} %bitcast.19, ...), custom_call_target="tpu_custom_call" | custom-call | flops 15032385536 | bytes 13631488 | tf_op jit(solution)/shard_map/encode/pallas_call | solution.py:51
  30.6 23.8 %all-to-all-done = bf16[16,128,512]{2,1,0:T(8,128)(2,1)} async-done(((bf16[16,128,512]{2,1,0:T(8,128)(2,1)}), bf16[16,128,512]{2,1,0:T(8,128)(2,1)}, u32[]{:S(2)}, u32[]{:S(2)}) %all-to-all-start) | async-done | bytes 2097184 | tf_op jit(solution)/shard_map/all_to_all | solution.py:200
  54.5 45.3 %attend.1 = (bf16[2048,512]{1,0:T(8,128)(2,1)S(1)}, bf16[2048,512]{1,0:T(8,128)(2,1)S(1)}) custom-call(s32[16,3]{1,0:T(8,128)S(1)} %copy.17.neighbors_ref, f32[8]{0:T(128)S(1)} %broadcast_multiply_fusion.scale_ref, bf16[2048,512]{1,0:T(8,128)(2,1)} %get-tuple-element.7.q_ref, bf16[2048,512]{1,0:T(8,128)(2,1)} %get-tuple-element.8.k_ref, ...), custom_call_target="tpu_custom_call" | custom-call | flops 4026531840 | bytes 12582912 | tf_op jit(solution)/shard_map/attend/pallas_call | solution.py:159
  99.8 0.4 maximum_bitcast_fusion
  100.2 97.0 %all_to_all.14 = bf16[16,2,1,128,512]{4,3,2,1,0:T(8,128)(2,1)S(1)} all-to-all(bf16[16,2,1,128,512]{4,3,2,1,0:T(8,128)(2,1)S(1)} %maximum_bitcast_fusion), channel_id=1, replica_groups=mesh['grp'=2,'bus'=16] {'bus'}, dimensions={0} | all-to-all | bytes 8388608 | tf_op jit(solution)/shard_map/all_to_all | solution.py:212
  197.1 2.3 %slice_bitcast_fusion = (bf16[16,128,512]{2,1,0:T(8,128)(2,1)}, bf16[16,128,512]{2,1,0:T(8,128)(2,1)}) fusion(bf16[2,16,1,128,512]{4,3,2,0,1:T(8,128)(2,1)S(1)} %bitcast.20), kind=kLoop, calls=%fused_computation.1 | loop fusion | bytes 8388608 | tf_op jit(solution)/shard_map/squeeze | solution.py:214
  (1 shorter events, 0.0 us)
Async XLA Ops:
  0.6 7.1 %copy-start.6 = (s32[16,3]{0,1:T(4,128)S(1)}, s32[16,3]{0,1:T(4,128)}, u32[]{:S(2)}) copy-start(s32[16,3]{0,1:T(4,128)} %param.20) | copy-start | bytes 580
  0.6 7.2 %copy-start.5 = (s32[2048]{0:T(1024)S(1)}, s32[2048]{0:T(1024)}, u32[]{:S(2)}) copy-start(s32[2048]{0:T(1024)} %param.15) | copy-start | bytes 24580
  0.7 7.6 %copy-start.7 = (f32[8]{0:T(128)S(1)}, f32[8]{0:T(128)}, u32[]{:S(2)}) copy-start(f32[8]{0:T(128)} %param.19) | copy-start | bytes 100
  0.7 7.6 %copy-start.1 = (bf16[1024,512]{1,0:T(8,128)(2,1)S(1)}, bf16[1024,512]{1,0:T(8,128)(2,1)}, u32[]{:S(2)}) copy-start(bf16[1024,512]{1,0:T(8,128)(2,1)} %wk_ref.1) | copy-start | bytes 3145732
  0.7 7.6 %copy-start = (bf16[1024,512]{1,0:T(8,128)(2,1)S(1)}, bf16[1024,512]{1,0:T(8,128)(2,1)}, u32[]{:S(2)}) copy-start(bf16[1024,512]{1,0:T(8,128)(2,1)} %wq_ref.1) | copy-start | bytes 3145732
  0.7 7.6 %copy-start.4 = (f32[1024]{0:T(1024)S(1)}, f32[1024]{0:T(1024)}, u32[]{:S(2)}) copy-start(f32[1024]{0:T(1024)} %param.14) | copy-start | bytes 12292
  0.7 7.6 %copy-start.3 = (bf16[24,1024]{1,0:T(8,128)(2,1)S(1)}, bf16[24,1024]{1,0:T(8,128)(2,1)}, u32[]{:S(2)}) copy-start(bf16[24,1024]{1,0:T(8,128)(2,1)} %table_ref.1) | copy-start | bytes 147460
  0.7 53.8 %all-to-all-start = ((bf16[16,128,512]{2,1,0:T(8,128)(2,1)}), bf16[16,128,512]{2,1,0:T(8,128)(2,1)}, u32[]{:S(2)}, u32[]{:S(2)}) async-start(bf16[16,128,512]{2,1,0:T(8,128)(2,1)} %param.21), calls=%async_computation | async-start | bytes 4194304 | tf_op jit(solution)/shard_map/all_to_all | solution.py:200
  8.3 1.2 copy-start.2

commit v2 on v1

v2 whole, which is shorter than its diff:
```python
import functools
import math

import jax
import jax.numpy as jnp
from jax import lax
from jax.experimental import pallas as pl
from jax.experimental.pallas import tpu as pltpu
from jax.sharding import PartitionSpec as P

EPSILON = 1e-05
NEG_FILL = -1e30
VMEM_LIMIT = 56 << 20
WEIGHT_COPIES = 1


def nt_dot(a, b):
    return lax.dot_general(a, b, (((1,), (1,)), ((), ())), preferred_element_type=jnp.float32)


def tn_dot(a, b):
    return lax.dot_general(a, b, (((0,), (0,)), ((), ())), preferred_element_type=jnp.float32)


def encode_kernel(
    hour_ref, order_ref, series_ref, table_ref, gain_ref, wq_ref, wk_ref, wv_ref, q_ref, k_ref, v_ref
):
    tile = order_ref.shape[0]
    buses = series_ref.shape[0]
    hours = table_ref.shape[0]
    pick = lax.broadcasted_iota(jnp.int32, (tile, buses), 1) == order_ref[...]
    ordered = jnp.dot(
        pick.astype(jnp.bfloat16), series_ref[...], preferred_element_type=jnp.float32
    )
    table = table_ref[...].astype(jnp.float32)
    is_hour = lax.broadcasted_iota(jnp.int32, (hours, 1), 0) == hour_ref[0]
    hour_row = jnp.sum(jnp.where(is_hour, table, 0.0), axis=0, keepdims=True)
    mixed = ordered + hour_row
    power = jnp.mean(mixed * mixed, axis=1, keepdims=True)
    normed = (mixed * lax.rsqrt(power + EPSILON) * gain_ref[...]).astype(jnp.bfloat16)
    for weight_ref, out_ref in ((wq_ref, q_ref), (wk_ref, k_ref), (wv_ref, v_ref)):
        out_ref[...] = jnp.dot(
            normed, weight_ref[...], preferred_element_type=jnp.float32
        ).astype(jnp.bfloat16)


def encode(series, hour_ids, hour_table, norm_gain, order, w_query, w_key, w_value, tile):
    buses, width = series.shape
    feat = w_query.shape[1]
    whole = lambda shape: pl.BlockSpec(shape, lambda i, *_: (0, 0))
    row_spec = pl.BlockSpec((tile, feat), lambda i, *_: (i, 0))
    out = jax.ShapeDtypeStruct((buses, feat), jnp.bfloat16)
    return pl.pallas_call(
        encode_kernel,
        grid_spec=pltpu.PrefetchScalarGridSpec(
            num_scalar_prefetch=1,
            grid=(buses // tile,),
            in_specs=[
                pl.BlockSpec((tile, 1), lambda i, *_: (i, 0)),
                whole((buses, width)),
                whole(hour_table.shape),
                whole((1, width)),
                whole((width, feat)),
                whole((width, feat)),
                whole((width, feat)),
            ],
            out_specs=[row_spec, row_spec, row_spec],
        ),
        out_shape=[out, out, out],
        compiler_params=pltpu.CompilerParams(vmem_limit_bytes=VMEM_LIMIT),
        cost_estimate=pl.CostEstimate(
            flops=2 * buses * width * (buses + 3 * feat),
            bytes_accessed=2 * (buses * width + 3 * width * feat + 3 * buses * feat),
            transcendentals=buses,
        ),
        name="encode",
    )(
        hour_ids,
        order.reshape(buses, 1),
        series,
        hour_table,
        norm_gain.reshape(1, width),
        w_query,
        w_key,
        w_value,
    )


def both_heads(x):
    first_half = lax.broadcasted_iota(jnp.int32, x.shape, 1) < x.shape[1] // 2
    zero = jnp.zeros_like(x)
    return jnp.concatenate([jnp.where(first_half, x, zero), jnp.where(first_half, zero, x)], 0)


def tile_at(ref, block, rows):
    return ref[block * rows : (block + 1) * rows, :]


def near_tiles(ref, block, rows):
    last = ref.shape[0] // rows - 1
    near = (max(block - 1, 0), block, min(block + 1, last))
    return jnp.concatenate([tile_at(ref, c, rows) for c in near], 0)


def head_scales(scale_ref, rows):
    pair = pl.program_id(0)
    col = lax.broadcasted_iota(jnp.int32, (1, 2 * rows), 1)
    return jnp.where(col < rows, scale_ref[2 * pair], scale_ref[2 * pair + 1])


def softmax_over_keys(raw, scale, neighbors_ref, block, rows):
    scale_log2 = scale * math.log2(math.e)
    read = [neighbors_ref[block, d] >= 0 for d in range(3)]
    tiles = [raw[d * rows : (d + 1) * rows] for d in range(3)]
    tops = [
        jnp.where(ok, jnp.max(tile, axis=0, keepdims=True) * scale_log2, NEG_FILL)
        for ok, tile in zip(read, tiles)
    ]
    row_max = jnp.maximum(jnp.maximum(tops[0], tops[1]), tops[2])
    powers = jnp.concatenate(
        [
            jnp.exp2(tile * scale_log2 - jnp.where(ok, row_max, -NEG_FILL))
            for ok, tile in zip(read, tiles)
        ],
        0,
    )
    return powers * (1.0 / jnp.sum(powers, axis=0, keepdims=True))


class KeySums:
    def __init__(self, out_ref, rows):
        self.out_ref, self.rows, self.open = out_ref, rows, [None, None]

    def store(self, block, value):
        self.out_ref[block * self.rows : (block + 1) * self.rows, :] = value.astype(jnp.bfloat16)

    def add(self, block, part):
        low, own, high = [part[d * self.rows : (d + 1) * self.rows] for d in range(3)]
        if block > 0:
            self.store(block - 1, self.open[0] + low)
            own = self.open[1] + own
        self.open = [own, high]

    def close(self, block):
        self.store(block, self.open[0])


def weights_kernel(rows, neighbors_ref, scale_ref, q_ref, k_ref, w_ref):
    blocks = q_ref.shape[0] // rows
    scale = head_scales(scale_ref, rows)

    def products(b):
        return nt_dot(near_tiles(k_ref, b, rows), both_heads(tile_at(q_ref, b, rows)))

    raw = products(0)
    for b in range(blocks):
        ahead = products(b + 1) if b + 1 < blocks else None
        weights = softmax_over_keys(raw, scale, neighbors_ref, b, rows)
        w_ref[0, b] = weights.astype(jnp.bfloat16)
        raw = ahead


def value_kernel(rows, *refs):
    *w_refs, g_ref, dv_ref = refs
    blocks = g_ref.shape[0] // rows
    held = w_refs[0].shape[1]
    sums = KeySums(dv_ref, rows)

    def products(b):
        g_two = both_heads(tile_at(g_ref, b, rows))
        return jnp.dot(w_refs[b // held][0, b % held], g_two, preferred_element_type=jnp.float32)

    part = products(0)
    for b in range(blocks):
        ahead = products(b + 1) if b + 1 < blocks else None
        sums.add(b, part)
        part = ahead
    sums.close(blocks - 1)


def key_kernel(rows, neighbors_ref, scale_ref, q_ref, k_ref, v_ref, g_ref, dk_ref):
    blocks = q_ref.shape[0] // rows
    half = q_ref.shape[1] // 2
    scale = head_scales(scale_ref, rows)
    sums = KeySums(dk_ref, rows)

    def products(b):
        q_two = both_heads(tile_at(q_ref, b, rows))
        g_two = both_heads(tile_at(g_ref, b, rows))
        values = near_tiles(v_ref, b, rows)
        raw = nt_dot(near_tiles(k_ref, b, rows), q_two)
        return q_two, values, raw, nt_dot(values, g_two)

    def normalise(b, found):
        q_two, values, raw, dweights = found
        weights = softmax_over_keys(raw, scale, neighbors_ref, b, rows)
        attended = tn_dot(values, weights.astype(jnp.bfloat16))
        return q_two, dweights, weights, attended.astype(jnp.bfloat16).astype(jnp.float32)

    def finish(b, found):
        q_two, dweights, weights, attended = found
        turned = tile_at(g_ref, b, rows).astype(jnp.float32).T
        row_dot = jnp.concatenate(
            [
                jnp.sum(turned[:half] * attended[:half, :rows], axis=0, keepdims=True),
                jnp.sum(turned[half:] * attended[half:, rows:], axis=0, keepdims=True),
            ],
            1,
        )
        dscores = (weights * (dweights - row_dot) * scale).astype(jnp.bfloat16)
        sums.add(b, jnp.dot(dscores, q_two, preferred_element_type=jnp.float32))

    one, two = products(0), None
    for b in range(blocks):
        ahead = products(b + 1) if b + 1 < blocks else None
        now = normalise(b, one)
        if two is not None:
            finish(b - 1, two)
        one, two = ahead, now
    finish(blocks - 1, two)
    sums.close(blocks - 1)


def copy_kernel(x_ref, out_ref):
    out_ref[...] = x_ref[...]


def copied(value):
    run = math.gcd(value.shape[0], 4)
    spec = pl.BlockSpec((value.shape[0] // run,) + value.shape[1:], lambda i: (i, 0, 0))
    return pl.pallas_call(
        copy_kernel,
        grid=(run,),
        in_specs=[spec],
        out_specs=spec,
        out_shape=jax.ShapeDtypeStruct(value.shape, value.dtype),
        compiler_params=pltpu.CompilerParams(vmem_limit_bytes=8 << 20),
        cost_estimate=pl.CostEstimate(flops=0, bytes_accessed=4 * value.size, transcendentals=0),
        name="settle",
    )(value)


def by_pair(kernel, name, rows, heads, scalars, arrays, out_shape, limit, dots, exps):
    buses, feat = arrays[-1].shape
    lanes = 2 * feat // heads
    lane_spec = pl.BlockSpec((buses, lanes), lambda p, *_: (0, p))
    whole, pieces = [], []
    for x in arrays:
        count = WEIGHT_COPIES if x.ndim > 2 else 1
        for i in range(count):
            whole.append(x)
            pieces.append(weights_spec(x.shape, count, i) if x.ndim > 2 else lane_spec)
    out_spec = weights_spec(out_shape, 1, 0) if len(out_shape) > 2 else lane_spec
    moved = sum(math.prod(x.shape) for x in arrays) + math.prod(out_shape)
    return pl.pallas_call(
        functools.partial(kernel, rows),
        grid_spec=pltpu.PrefetchScalarGridSpec(
            num_scalar_prefetch=len(scalars),
            grid=(heads // 2,),
            in_specs=pieces,
            out_specs=out_spec,
        ),
        out_shape=pltpu.HBM(out_shape, jnp.bfloat16),
        compiler_params=pltpu.CompilerParams(vmem_limit_bytes=limit),
        cost_estimate=pl.CostEstimate(
            flops=2 * dots * 3 * rows * buses * feat,
            bytes_accessed=2 * moved,
            transcendentals=exps * 3 * rows * buses * heads,
        ),
        name=name,
    )(*scalars, *whole)


def weights_spec(shape, count, at):
    return pl.BlockSpec((1, shape[1] // count) + shape[2:], lambda p, *_: (p, at, 0, 0))


def on_device(
    series,
    hour_ids,
    hour_table,
    norm_gain,
    bus_order,
    w_query,
    w_key,
    w_value,
    score_scale,
    neighbors,
    grad_out,
):
    head_count = score_scale.shape[0]
    snap_count, block_rows, feat_width = grad_out.shape
    own_snaps, bus_count, _ = series.shape
    devices = lax.axis_size("bus")
    head_scale = score_scale / math.sqrt(feat_width // head_count)

    def exchange(value):
        return lax.all_to_all(value, "bus", split_axis=0, concat_axis=0, tiled=True)

    def give_back(pieces):
        value = jnp.stack([piece.reshape(devices, block_rows, feat_width) for piece in pieces], 1)
        return exchange(value).reshape(snap_count, block_rows, feat_width)

    grads = exchange(grad_out.reshape(devices, own_snaps, block_rows, feat_width))
    scalars = (neighbors, head_scale)
    shape = (bus_count, feat_width)
    weight_shape = (head_count // 2, bus_count // block_rows, 3 * block_rows, 2 * block_rows)
    value_grads, key_grads = [], []
    for s in range(own_snaps):
        queries, keys, values = encode(
            series[s], hour_ids[s : s + 1], hour_table, norm_gain, bus_order,
            w_query, w_key, w_value, math.gcd(bus_count, 256),
        )
        weights = by_pair(
            weights_kernel, "weights", block_rows, head_count, scalars, (queries, keys),
            weight_shape, VMEM_LIMIT, 1, 1,
        )
        own_grads = grads[:, s].reshape(shape)
        value_grads.append(
            by_pair(
                value_kernel, "value_grad", block_rows, head_count, (),
                (weights, own_grads),
                shape, 52 << 20, 1, 0,
            )
        )
        own_grads, _ = lax.optimization_barrier((own_grads, value_grads[-1]))
        key_grads.append(
            by_pair(
                key_kernel, "key_grad", block_rows, head_count, scalars,
                (queries, keys, values, own_grads), shape, VMEM_LIMIT, 4, 1,
            )
        )
    value_grad = give_back(value_grads)
    value_grad, key_grads = lax.optimization_barrier((value_grad, key_grads))
    key_grad = give_back(key_grads)
    return (key_grad, copied(value_grad))


def solution(mesh):
    return jax.shard_map(
        on_device,
        mesh=mesh,
        in_specs=(
            P(("grp", "bus"), None, None),
            P(("grp", "bus")),
            P(),
            P(),
            P("grp"),
            P(),
            P(),
            P(),
            P(),
            P("grp", None),
            P("grp", "bus", None),
        ),
        out_specs=(P("grp", "bus", None), P("grp", "bus", None)),
        check_vma=False,
    )
```

time: 201 us -> 173 us (0.86)
  blocking collectives: 97 us -> 0 us
  waiting for transfers between devices: 23.8 us -> 78.1 us
  starting transfers between devices: 6.38 us -> 16.5 us
  Pallas kernels: 66.4 us -> 68.9 us
  local copies, waits for them, and re-layouts: 3.98 us -> 6.44 us
    all_to_all x1 -> x0, blocking collectives: 97 us -> none  [on_device(): back = lax.all_to_all(both, 'bus', split_axis=0, concat_axis=0, tiled=True)]
    all_to_all x1 -> x3, waiting for transfers between devices: 23.8 us -> 78.1 us  [exchange(): return lax.all_to_all(value, 'bus', split_axis=0, concat_axis=0, tiled=True)]
    all_to_all x1 -> x3, starting transfers between devices: 6.38 us -> 16.5 us  [exchange(): return lax.all_to_all(value, 'bus', split_axis=0, concat_axis=0, tiled=True)]
    unnamed x17 -> x10, local copies, waits for them, and re-layouts: 1.33 us -> 5.09 us
    squeeze x1 -> x0, local copies, waits for them, and re-layouts: 2.28 us -> none  [on_device(): return (back[0], back[1])]
    pallas_call x1 -> x4, Pallas kernels: 45.3 us -> 46.6 us  [the longest x3 44.8 us: by_pair(): pl.pallas_call(functools.partial(kernel, rows), grid_spec=pltpu.PrefetchS...]
  transfers between devices with their start and end apart: 1 -> 3, of which waited for: 1 -> 3; matrix products, arithmetic and copies ran while one was open for 0% -> 1% of each run, Pallas kernels for 11% -> 35%
where the time goes in v2:
time: 173 us; the launch traced here: 172 us
  waiting for transfers between devices  78.1 us (45%)
  Pallas kernels  68.9 us (40%)
  starting transfers between devices  16.5 us (10%)
  local copies, waits for them, and re-layouts  6.44 us (4%)
    all_to_all x3, waiting for transfers between devices, exchange(): return lax.all_to_all(value, 'bus', split_axis=0, concat_axis=0, tiled=True)  78.1 us
    pallas_call x3, Pallas kernels, by_pair(): pl.pallas_call(functools.partial(kernel, rows), grid_spec=pltpu.PrefetchS...  44.8 us
    pallas_call x1, Pallas kernels, encode(): pl.pallas_call(encode_kernel, grid_spec=pltpu.PrefetchScalarGridSpec(num_...  22.2 us
    all_to_all x3, starting transfers between devices, exchange(): return lax.all_to_all(value, 'bus', split_axis=0, concat_axis=0, tiled=True)  16.5 us
    unnamed x10, local copies, waits for them, and re-layouts  5.09 us
  transfers between devices with their start and end apart: 3, of which 3 were waited for; matrix products, arithmetic and copies ran while one was open for 1% of the time, Pallas kernels for 35%

profile of v2, /device:TPU:12, one launch (start us, length us, event | category | flops | bytes accessed | tf_op | source)
XLA Modules:
  0.0 171.8 jit_solution(1811163528956020226)
XLA Ops:
  0.6 0.0 copy-start.2
  0.6 0.0 copy-start.1
  0.7 0.0 copy-start.3
  0.7 6.4 %all-to-all-start = ((bf16[16,1,128,512]{3,2,1,0:T(8,128)(2,1)}), bf16[16,1,128,512]{3,2,1,0:T(8,128)(2,1)S(1)}, u32[]{:S(2)}, u32[]{:S(2)}) async-start(bf16[16,1,128,512]{3,2,1,0:T(8,128)(2,1)} %bitcast.17), calls=%async_computation | async-start | bytes 4194304 | tf_op jit(solution)/shard_map/all_to_all | solution.py:298
  7.7 0.0 copy-done.2
  7.7 0.7 copy.19.neighbors_ref
  8.4 0.0 copy-done.1
  8.4 1.4 copy.18.order_ref
  9.7 0.0 copy-done.3
  9.7 0.5 broadcast_multiply_fusion.scale_ref
  10.3 22.2 %encode.1 = (bf16[2048,512]{1,0:T(8,128)(2,1)}, bf16[2048,512]{1,0:T(8,128)(2,1)}, bf16[2048,512]{1,0:T(8,128)(2,1)}) custom-call(s32[1]{0:T(128)S(6)} %copy.24.hour_ref, s32[2048,1]{1,0:T(8,128)} %copy.18.order_ref, bf16[2048,1024]{1,0:T(8,128)(2,1)} %bitcast.20, bf16[24,1024]{1,0:T(8,128)(2,1)} %table_ref.1, f32[1,1024]{1,0:T(1,128)} %bitcast.21, ...), custom_call_target="tpu_custom_call" | custom-call | flops 15032385536 | bytes 13631488 | tf_op jit(solution)/shard_map/encode/pallas_call | solution.py:53
  32.5 14.1 %weights.1.refs_0_ = bf16[4,16,384,256]{3,2,1,0:T(8,128)(2,1)} custom-call(s32[16,3]{1,0:T(8,128)} %copy.19.neighbors_ref, f32[8]{0:T(128)} %broadcast_multiply_fusion.scale_ref, bf16[2048,512]{1,0:T(8,128)(2,1)} %get-tuple-element.8.q_ref, bf16[2048,512]{1,0:T(8,128)(2,1)} %get-tuple-element.9.k_ref), custom_call_target="tpu_custom_call" | custom-call | flops 805306368 | bytes 16777216 | tf_op jit(solution)/shard_map/weights/pallas_call | solution.py:255
  46.6 7.7 %all-to-all-done = bf16[16,1,128,512]{3,2,1,0:T(8,128)(2,1)S(1)} async-done(((bf16[16,1,128,512]{3,2,1,0:T(8,128)(2,1)}), bf16[16,1,128,512]{3,2,1,0:T(8,128)(2,1)S(1)}, u32[]{:S(2)}, u32[]{:S(2)}) %all-to-all-start) | async-done | bytes 2097184 | tf_op jit(solution)/shard_map/all_to_all | solution.py:298
  54.3 0.0 copy-start
  54.3 1.3 copy-done
  55.6 8.3 %value_grad.1 = bf16[2048,512]{1,0:T(8,128)(2,1)} custom-call(bf16[4,16,384,256]{3,2,1,0:T(8,128)(2,1)} %weights.1.refs_0_, bf16[2048,512]{1,0:T(8,128)(2,1)} %bitcast.14), custom_call_target="tpu_custom_call" | custom-call | flops 805306368 | bytes 16777216 | tf_op jit(solution)/shard_map/value_grad/pallas_call | solution.py:255
  64.0 5.1 %all-to-all-start.1 = ((bf16[16,1,128,512]{3,2,1,0:T(8,128)(2,1)}), bf16[16,1,128,512]{3,2,1,0:T(8,128)(2,1)S(1)}, u32[]{:S(2)}, u32[]{:S(2)}) async-start(bf16[16,1,128,512]{3,2,1,0:T(8,128)(2,1)} %bitcast.16), calls=%async_computation.1 | async-start | bytes 4194304 | tf_op jit(solution)/shard_map/all_to_all | solution.py:298
  69.0 22.4 %key_grad.1 = bf16[2048,512]{1,0:T(8,128)(2,1)} custom-call(s32[16,3]{1,0:T(8,128)} %copy.19.neighbors_ref, f32[8]{0:T(128)} %broadcast_multiply_fusion.scale_ref, bf16[2048,512]{1,0:T(8,128)(2,1)} %get-tuple-element.8.q_ref, bf16[2048,512]{1,0:T(8,128)(2,1)} %get-tuple-element.9.k_ref, bf16[2048,512]{1,0:T(8,128)(2,1)} %get-tuple-element.10.v_ref, ...), custom_call_target="tpu_custom_call" | custom-call | flops 3221225472 | bytes 10485760 | tf_op jit(solution)/shard_map/key_grad/pallas_call | solution.py:255
  91.4 24.9 %all-to-all-done.1 = bf16[16,1,128,512]{3,2,1,0:T(8,128)(2,1)S(1)} async-done(((bf16[16,1,128,512]{3,2,1,0:T(8,128)(2,1)}), bf16[16,1,128,512]{3,2,1,0:T(8,128)(2,1)S(1)}, u32[]{:S(2)}, u32[]{:S(2)}) %all-to-all-start.1) | async-done | bytes 2097184 | tf_op jit(solution)/shard_map/all_to_all | solution.py:298
  116.3 5.1 %all-to-all-start.2 = ((bf16[16,1,128,512]{3,2,1,0:T(8,128)(2,1)}), bf16[16,1,128,512]{3,2,1,0:T(8,128)(2,1)}, u32[]{:S(2)}, u32[]{:S(2)}) async-start(bf16[16,1,128,512]{3,2,1,0:T(8,128)(2,1)} %bitcast.18), calls=%async_computation.2 | async-start | bytes 4194304 | tf_op jit(solution)/shard_map/all_to_all | solution.py:298
  121.3 1.8 %settle.1 = bf16[16,128,512]{2,1,0:T(8,128)(2,1)} custom-call(bf16[16,128,512]{2,1,0:T(8,128)(2,1)S(1)} %bitcast.13), custom_call_target="tpu_custom_call" | custom-call | bytes 4194304 | tf_op jit(solution)/shard_map/settle/pallas_call | solution.py:231
  123.2 45.5 %all-to-all-done.2 = bf16[16,1,128,512]{3,2,1,0:T(8,128)(2,1)} async-done(((bf16[16,1,128,512]{3,2,1,0:T(8,128)(2,1)}), bf16[16,1,128,512]{3,2,1,0:T(8,128)(2,1)}, u32[]{:S(2)}, u32[]{:S(2)}) %all-to-all-start.2) | async-done | bytes 2097184 | tf_op jit(solution)/shard_map/all_to_all | solution.py:298
  168.7 3.1 %copy.25 = bf16[16,128,512]{2,1,0:T(8,128)(2,1)} copy(bf16[16,128,512]{2,1,0:T(8,128)(2,1)} %bitcast.10) | data formatting | bytes 4194304
Async XLA Ops:
  0.6 7.1 %copy-start.2 = (s32[16,3]{0,1:T(4,128)S(1)}, s32[16,3]{0,1:T(4,128)}, u32[]{:S(2)}) copy-start(s32[16,3]{0,1:T(4,128)} %param.20) | copy-start | bytes 580
  0.6 7.8 %copy-start.1 = (s32[2048]{0:T(1024)S(1)}, s32[2048]{0:T(1024)}, u32[]{:S(2)}) copy-start(s32[2048]{0:T(1024)} %param.15) | copy-start | bytes 24580
  0.7 9.1 %copy-start.3 = (f32[8]{0:T(128)S(1)}, f32[8]{0:T(128)}, u32[]{:S(2)}) copy-start(f32[8]{0:T(128)} %param.19) | copy-start | bytes 100
  0.7 53.7 %all-to-all-start = ((bf16[16,1,128,512]{3,2,1,0:T(8,128)(2,1)}), bf16[16,1,128,512]{3,2,1,0:T(8,128)(2,1)S(1)}, u32[]{:S(2)}, u32[]{:S(2)}) async-start(bf16[16,1,128,512]{3,2,1,0:T(8,128)(2,1)} %bitcast.17), calls=%async_computation | async-start | bytes 4194304 | tf_op jit(solution)/shard_map/all_to_all | solution.py:298
  54.3 1.3 copy-start
  64.0 52.3 %all-to-all-start.1 = ((bf16[16,1,128,512]{3,2,1,0:T(8,128)(2,1)}), bf16[16,1,128,512]{3,2,1,0:T(8,128)(2,1)S(1)}, u32[]{:S(2)}, u32[]{:S(2)}) async-start(bf16[16,1,128,512]{3,2,1,0:T(8,128)(2,1)} %bitcast.16), calls=%async_computation.1 | async-start | bytes 4194304 | tf_op jit(solution)/shard_map/all_to_all | solution.py:298
  116.3 52.4 %all-to-all-start.2 = ((bf16[16,1,128,512]{3,2,1,0:T(8,128)(2,1)}), bf16[16,1,128,512]{3,2,1,0:T(8,128)(2,1)}, u32[]{:S(2)}, u32[]{:S(2)}) async-start(bf16[16,1,128,512]{3,2,1,0:T(8,128)(2,1)} %bitcast.18), calls=%async_computation.2 | async-start | bytes 4194304 | tf_op jit(solution)/shard_map/all_to_all | solution.py:298

commit v3 on v2

v3 whole, which is shorter than its diff:
```python
import functools
import math

import jax
import jax.numpy as jnp
from jax import lax
from jax.experimental import pallas as pl
from jax.experimental.pallas import tpu as pltpu
from jax.sharding import PartitionSpec as P

EPSILON = 1e-05
NEG_FILL = -1e30
VMEM_LIMIT = 56 << 20
SETTLE_STEPS = 4
EARLY_PAIRS = 2
PLANE = 4


def nt_dot(a, b):
    return lax.dot_general(a, b, (((1,), (1,)), ((), ())), preferred_element_type=jnp.float32)


def tn_dot(a, b):
    return lax.dot_general(a, b, (((0,), (0,)), ((), ())), preferred_element_type=jnp.float32)


def encode_kernel(
    hour_ref, order_ref, series_ref, table_ref, gain_ref, wq_ref, wk_ref, wv_ref, q_ref, k_ref, v_ref
):
    tile = order_ref.shape[0]
    buses = series_ref.shape[0]
    hours = table_ref.shape[0]
    pick = lax.broadcasted_iota(jnp.int32, (tile, buses), 1) == order_ref[...]
    ordered = jnp.dot(
        pick.astype(jnp.bfloat16), series_ref[...], preferred_element_type=jnp.float32
    )
    table = table_ref[...].astype(jnp.float32)
    is_hour = lax.broadcasted_iota(jnp.int32, (hours, 1), 0) == hour_ref[0]
    hour_row = jnp.sum(jnp.where(is_hour, table, 0.0), axis=0, keepdims=True)
    mixed = ordered + hour_row
    power = jnp.mean(mixed * mixed, axis=1, keepdims=True)
    normed = (mixed * lax.rsqrt(power + EPSILON) * gain_ref[...]).astype(jnp.bfloat16)
    for weight_ref, out_ref in ((wq_ref, q_ref), (wk_ref, k_ref), (wv_ref, v_ref)):
        out_ref[...] = jnp.dot(
            normed, weight_ref[...], preferred_element_type=jnp.float32
        ).astype(jnp.bfloat16)


def encode(series, hour_ids, hour_table, norm_gain, order, w_query, w_key, w_value, tile):
    buses, width = series.shape
    feat = w_query.shape[1]
    whole = lambda shape: pl.BlockSpec(shape, lambda i, *_: (0, 0))
    row_spec = pl.BlockSpec((tile, feat), lambda i, *_: (i, 0))
    out = jax.ShapeDtypeStruct((buses, feat), jnp.bfloat16)
    return pl.pallas_call(
        encode_kernel,
        grid_spec=pltpu.PrefetchScalarGridSpec(
            num_scalar_prefetch=1,
            grid=(buses // tile,),
            in_specs=[
                pl.BlockSpec((tile, 1), lambda i, *_: (i, 0)),
                whole((buses, width)),
                whole(hour_table.shape),
                whole((1, width)),
                whole((width, feat)),
                whole((width, feat)),
                whole((width, feat)),
            ],
            out_specs=[row_spec, row_spec, row_spec],
        ),
        out_shape=[out, out, out],
        compiler_params=pltpu.CompilerParams(vmem_limit_bytes=VMEM_LIMIT),
        cost_estimate=pl.CostEstimate(
            flops=2 * buses * width * (buses + 3 * feat),
            bytes_accessed=2 * (buses * width + 3 * width * feat + 3 * buses * feat),
            transcendentals=buses,
        ),
        name="encode",
    )(
        hour_ids,
        order.reshape(buses, 1),
        series,
        hour_table,
        norm_gain.reshape(1, width),
        w_query,
        w_key,
        w_value,
    )


def both_heads(x):
    first_half = lax.broadcasted_iota(jnp.int32, x.shape, 1) < x.shape[1] // 2
    zero = jnp.zeros_like(x)
    return jnp.concatenate([jnp.where(first_half, x, zero), jnp.where(first_half, zero, x)], 0)


def tile_at(ref, block, rows):
    return ref[block * rows : (block + 1) * rows, :]


def near_tiles(ref, block, rows):
    last = ref.shape[0] // rows - 1
    near = (max(block - 1, 0), block, min(block + 1, last))
    return jnp.concatenate([tile_at(ref, c, rows) for c in near], 0)


def head_scales(scale_ref, rows):
    pair = pl.program_id(0)
    col = lax.broadcasted_iota(jnp.int32, (1, 2 * rows), 1)
    return jnp.where(col < rows, scale_ref[2 * pair], scale_ref[2 * pair + 1])


def softmax_over_keys(raw, scale, neighbors_ref, block, rows):
    scale_log2 = scale * math.log2(math.e)
    read = [neighbors_ref[block, d] >= 0 for d in range(3)]
    tiles = [raw[d * rows : (d + 1) * rows] for d in range(3)]
    tops = [
        jnp.where(ok, jnp.max(tile, axis=0, keepdims=True) * scale_log2, NEG_FILL)
        for ok, tile in zip(read, tiles)
    ]
    row_max = jnp.maximum(jnp.maximum(tops[0], tops[1]), tops[2])
    powers = jnp.concatenate(
        [
            jnp.exp2(tile * scale_log2 - jnp.where(ok, row_max, -NEG_FILL))
            for ok, tile in zip(read, tiles)
        ],
        0,
    )
    total = jnp.sum(powers, axis=0, keepdims=True)
    return powers * (1.0 / total), row_max + jnp.log2(total)


class KeySums:
    def __init__(self, out_ref, rows, flip=None):
        self.out_ref, self.rows, self.flip, self.open = out_ref, rows, flip, [None, None]

    def store(self, block, value):
        start = block * self.rows
        if self.flip is not None:
            start = pl.multiple_of((self.flip ^ block) * self.rows, self.rows)
        self.out_ref[pl.ds(start, self.rows), :] = value.astype(jnp.bfloat16)

    def add(self, block, part):
        low, own, high = [part[d * self.rows : (d + 1) * self.rows] for d in range(3)]
        if block > 0:
            self.store(block - 1, self.open[0] + low)
            own = self.open[1] + own
        self.open = [own, high]

    def close(self, block):
        self.store(block, self.open[0])


def weights_kernel(
    rows, neighbors_ref, scale_ref, q_ref, k_ref, v_ref, w_ref, attended_ref, shift_ref
):
    blocks = q_ref.shape[0] // rows
    scale = head_scales(scale_ref, rows)

    def products(b):
        return nt_dot(near_tiles(k_ref, b, rows), both_heads(tile_at(q_ref, b, rows)))

    def attend(b, weights_b):
        attended = tn_dot(near_tiles(v_ref, b, rows), weights_b)
        attended_ref[0, b] = attended.astype(jnp.bfloat16)

    raw, last = products(0), None
    for b in range(blocks):
        ahead = products(b + 1) if b + 1 < blocks else None
        weights, shift = softmax_over_keys(raw, scale, neighbors_ref, b, rows)
        weights_b = weights.astype(jnp.bfloat16)
        w_ref[0, b] = weights_b
        shift_ref[0, b : b + 1] = shift
        if last is not None:
            attend(b - 1, last)
        raw, last = ahead, weights_b
    attend(blocks - 1, last)


def flipped_value_kernel(rows, me_ref, *refs):
    value_kernel(rows, *refs, flip=me_ref[0])


def value_kernel(rows, w_ref, g_ref, *rest, flip=None):
    dv_ref = rest[-1]
    blocks = g_ref.shape[0] // rows
    sums = KeySums(dv_ref, rows, flip)

    def products(b):
        g_two = both_heads(tile_at(g_ref, b, rows))
        return jnp.dot(w_ref[0, b], g_two, preferred_element_type=jnp.float32)

    part = products(0)
    for b in range(blocks):
        ahead = products(b + 1) if b + 1 < blocks else None
        sums.add(b, part)
        part = ahead
    sums.close(blocks - 1)


def key_kernel(
    rows, neighbors_ref, scale_ref, q_ref, k_ref, v_ref, g_ref, attended_ref, shift_ref, *rest
):
    dk_ref = rest[-1]
    blocks = q_ref.shape[0] // rows
    half = q_ref.shape[1] // 2
    scale = head_scales(scale_ref, rows)
    scale_log2 = scale * math.log2(math.e)
    sums = KeySums(dk_ref, rows)

    def products(b):
        q_two = both_heads(tile_at(q_ref, b, rows))
        g_two = both_heads(tile_at(g_ref, b, rows))
        raw = nt_dot(near_tiles(k_ref, b, rows), q_two)
        return q_two, raw, nt_dot(near_tiles(v_ref, b, rows), g_two)

    def finish(b, found):
        q_two, raw, dweights = found
        shift = shift_ref[0, b : b + 1]
        weights = jnp.concatenate(
            [
                jnp.exp2(
                    raw[d * rows : (d + 1) * rows] * scale_log2
                    - jnp.where(neighbors_ref[b, d] >= 0, shift, -NEG_FILL)
                )
                for d in range(3)
            ],
            0,
        )
        turned = tile_at(g_ref, b, rows).astype(jnp.float32).T
        attended = attended_ref[0, b].astype(jnp.float32)
        row_dot = jnp.concatenate(
            [
                jnp.sum(turned[:half] * attended[:half, :rows], axis=0, keepdims=True),
                jnp.sum(turned[half:] * attended[half:, rows:], axis=0, keepdims=True),
            ],
            1,
        )
        dscores = (weights * (dweights - row_dot) * scale).astype(jnp.bfloat16)
        return jnp.dot(dscores, q_two, preferred_element_type=jnp.float32)

    one, part = products(0), None
    for b in range(blocks):
        ahead = products(b + 1) if b + 1 < blocks else None
        now = finish(b, one)
        if part is not None:
            sums.add(b - 1, part)
        one, part = ahead, now
    sums.add(blocks - 1, part)
    sums.close(blocks - 1)


def settle_kernel(me_ref, x_ref, out_ref):
    out_ref[...] = x_ref[...]


def settle(me, swapped, feat):
    devices, rows, lanes = swapped.shape
    block = (1, rows, lanes)
    return pl.pallas_call(
        settle_kernel,
        grid_spec=pltpu.PrefetchScalarGridSpec(
            num_scalar_prefetch=1,
            grid=(devices,),
            in_specs=[pl.BlockSpec(block, lambda j, me_ref: (j, 0, 0))],
            out_specs=pl.BlockSpec(block, lambda j, me_ref: (me_ref[0] ^ j, 0, 0)),
        ),
        out_shape=pltpu.HBM((devices, rows, feat), jnp.bfloat16),
        compiler_params=pltpu.CompilerParams(vmem_limit_bytes=8 << 20),
        cost_estimate=pl.CostEstimate(flops=0, bytes_accessed=4 * swapped.size, transcendentals=0),
        name="settle",
    )(me, swapped)


def swap(value, bits):
    devices = lax.axis_size("bus")
    return lax.ppermute(value, "bus", [(i, i ^ bits) for i in range(devices)])


def swap_far(parts):
    devices = parts.shape[0]
    planes = devices // PLANE

    far = [parts[:PLANE]]
    far += [swap(parts[PLANE * k : PLANE * (k + 1)], PLANE * k) for k in range(1, planes)]
    return far


def swap_near(far):
    planes = len(far)
    up = swap(jnp.stack([entry[2:] for entry in far]), 2)
    right = swap(jnp.stack([jnp.stack([entry[1] for entry in far]), up[:, 1]], 1), 1)
    order = []
    for k in range(planes):
        order += [far[k][0], right[k, 0], up[k, 0], right[k, 1]]
    return jnp.stack(order)


def part_kernel(late_ref, _, dk_ref, dv_ref):
    lanes = dv_ref.shape[2]
    dv_ref[...] = late_ref[:, :, :lanes]
    dk_ref[...] = late_ref[:, :, lanes:]


def part(late, settled):
    devices, rows, feat = settled.shape
    width = late.shape[2]
    run = devices // math.gcd(devices, SETTLE_STEPS)
    out = pltpu.HBM(settled.shape, jnp.bfloat16)
    whole = pl.BlockSpec((run, rows, feat), lambda i: (i, 0, 0))
    last = (2 * feat - width) // (width - feat)
    return pl.pallas_call(
        part_kernel,
        grid=(devices // run,),
        in_specs=[
            pl.BlockSpec((run, rows, width), lambda i: (i, 0, 0)),
            pl.BlockSpec(memory_space=pl.ANY),
        ],
        out_specs=[whole, pl.BlockSpec((run, rows, width - feat), lambda i: (i, 0, last))],
        out_shape=[out, out],
        input_output_aliases={1: 1},
        compiler_params=pltpu.CompilerParams(vmem_limit_bytes=24 << 20),
        cost_estimate=pl.CostEstimate(flops=0, bytes_accessed=4 * late.size, transcendentals=0),
        name="part",
    )(late, settled)


def by_pair(
    kernel, name, rows, heads, feat, first, count, scalars, arrays, outs, out_first, dots, exps,
    into=None, limit=50,
):
    buses, lanes = arrays[1].shape[0], 2 * feat // heads

    def spec(shape, at):
        if len(shape) > 2:
            zeros = (0,) * (len(shape) - 1)
            return pl.BlockSpec((1,) + shape[1:], lambda p, *_: (at + p, *zeros))
        return pl.BlockSpec((buses, lanes), lambda p, *_: (0, at + p))

    specs = [spec(x.shape, first) for x in arrays]
    arrays, alias = list(arrays), {}
    if into is not None:
        alias = {len(scalars) + len(arrays): 0}
        specs.append(pl.BlockSpec(memory_space=pl.ANY))
        arrays.append(into)
    return pl.pallas_call(
        functools.partial(kernel, rows),
        grid_spec=pltpu.PrefetchScalarGridSpec(
            num_scalar_prefetch=len(scalars),
            grid=(count,),
            in_specs=specs,
            out_specs=[spec(x.shape, out_first) for x in outs],
        ),
        out_shape=[pltpu.HBM(x.shape, x.dtype) for x in outs],
        input_output_aliases=alias,
        compiler_params=pltpu.CompilerParams(vmem_limit_bytes=limit << 20),
        cost_estimate=pl.CostEstimate(
            flops=2 * dots * 3 * rows * buses * count * lanes,
            bytes_accessed=2 * count * heads // 2 * sum(math.prod(x.shape) for x in arrays),
            transcendentals=exps * 3 * rows * buses * 2 * count,
        ),
        name=name,
    )(*scalars, *arrays)


def on_device(
    series,
    hour_ids,
    hour_table,
    norm_gain,
    bus_order,
    w_query,
    w_key,
    w_value,
    score_scale,
    neighbors,
    grad_out,
):
    head_count = score_scale.shape[0]
    snap_count, block_rows, feat_width = grad_out.shape
    bus_count = series.shape[1]
    devices = lax.axis_size("bus")
    head_scale = score_scale / math.sqrt(feat_width // head_count)
    pairs, lanes = head_count // 2, 2 * feat_width // head_count
    early = EARLY_PAIRS
    me = lax.axis_index("bus").astype(jnp.int32).reshape(1)
    late = pairs - early

    def exchange(value):
        return lax.all_to_all(value, "bus", split_axis=0, concat_axis=0, tiled=True)

    def blocks_of(value):
        return value.reshape(devices, block_rows, value.shape[-1])

    scalars = (neighbors, head_scale)
    bus_blocks = bus_count // block_rows
    bf16 = lambda *shape: jax.ShapeDtypeStruct(shape, jnp.bfloat16)
    call = functools.partial(by_pair, rows=block_rows, heads=head_count, feat=feat_width)

    grads = exchange(grad_out).reshape(bus_count, feat_width)
    queries, keys, values = encode(
        series[0], hour_ids, hour_table, norm_gain, bus_order,
        w_query, w_key, w_value, math.gcd(bus_count, 256),
    )
    weights, attended, shifts = call(
        weights_kernel, "weights", limit=56, first=0, count=pairs, scalars=scalars,
        arrays=(queries, keys, values), out_first=0, dots=2, exps=1,
        outs=[
            bf16(pairs, bus_blocks, 3 * block_rows, 2 * block_rows),
            bf16(pairs, bus_blocks, lanes, 2 * block_rows),
            jax.ShapeDtypeStruct((pairs, bus_blocks, 2 * block_rows), jnp.float32),
        ],
    )
    (early_value,) = call(
        flipped_value_kernel, "value_early", first=0, count=early, scalars=(me,),
        arrays=(weights, grads), outs=[bf16(bus_count, early * lanes)], out_first=0,
        dots=1, exps=0,
    )
    early_far = swap_far(blocks_of(early_value))
    grads, _ = lax.optimization_barrier((grads, early_value))
    rest_out = bf16(bus_count, late * lanes + feat_width)
    (rest,) = call(
        value_kernel, "value_late", first=early, count=late, scalars=(),
        arrays=(weights, grads), outs=[rest_out], out_first=0, dots=1, exps=0,
    )
    (rest,) = call(
        key_kernel, "key", first=0, count=pairs, scalars=scalars,
        arrays=(queries, keys, values, grads, attended, shifts), outs=[rest_out],
        out_first=late, dots=3, exps=1, into=rest,
    )
    early_far, rest = lax.optimization_barrier((early_far, rest))
    late_out = exchange(blocks_of(rest))
    early_out = swap_near(early_far)
    return tuple(part(late_out, settle(me, early_out, feat_width)))


def solution(mesh):
    return jax.shard_map(
        on_device,
        mesh=mesh,
        in_specs=(
            P(("grp", "bus"), None, None),
            P(("grp", "bus")),
            P(),
            P(),
            P("grp"),
            P(),
            P(),
            P(),
            P(),
            P("grp", None),
            P("grp", "bus", None),
        ),
        out_specs=(P("grp", "bus", None), P("grp", "bus", None)),
        check_vma=False,
    )
```

time: 173 us -> 164 us (0.948)
  waiting for transfers between devices: 78.1 us -> 66.6 us
  Pallas kernels: 68.9 us -> 71.1 us
    all_to_all x3 -> x2, waiting for transfers between devices: 78.1 us -> 37.6 us  [exchange(): return lax.all_to_all(value, 'bus', split_axis=0, concat_axis=0, tiled=True)]
    ppermute x0 -> x5, waiting for transfers between devices: none -> 29 us  [swap(): return lax.ppermute(value, 'bus', [(i, i ^ bits) for i in range(devices)])]
    pallas_call x1 -> x2, Pallas kernels: 1.85 us -> 7.24 us  [the longest x1 5.12 us: settle(): pl.pallas_call(settle_kernel, grid_spec=pltpu.PrefetchScalarGridSpec(num_...]
    ppermute x0 -> x5, starting transfers between devices: none -> 5.21 us  [swap(): return lax.ppermute(value, 'bus', [(i, i ^ bits) for i in range(devices)])]
    all_to_all x3 -> x2, starting transfers between devices: 16.5 us -> 11.8 us  [exchange(): return lax.all_to_all(value, 'bus', split_axis=0, concat_axis=0, tiled=True)]
    unnamed x10 -> x43, local copies, waits for them, and re-layouts: 5.09 us -> 1.64 us
    pallas_call x3 -> x4, Pallas kernels: 44.8 us -> 41.6 us  [by_pair(): pl.pallas_call(functools.partial(kernel, rows), grid_spec=pltpu.PrefetchS...]
    another operation x0 -> x3, local copies, waits for them, and re-layouts: none -> 1.97 us  [the longest x2 1.96 us: swap_near(): up = swap(jnp.stack([entry[2:] for entry in far]), 2)]
  transfers between devices with their start and end apart: 3 -> 7, of which waited for: 3 -> 4; matrix products, arithmetic and copies ran while one was open for 1% -> 3% of each run, Pallas kernels for 35% -> 39%
where the time goes in v3:
time: 164 us; the launch traced here: 163 us
  Pallas kernels  71.1 us (43%)
  waiting for transfers between devices  66.6 us (41%)
  starting transfers between devices  17 us (10%)
  local copies, waits for them, and re-layouts  6.26 us (4%)
    pallas_call x4, Pallas kernels, by_pair(): pl.pallas_call(functools.partial(kernel, rows), grid_spec=pltpu.PrefetchS...  41.6 us
    all_to_all x2, waiting for transfers between devices, exchange(): return lax.all_to_all(value, 'bus', split_axis=0, concat_axis=0, tiled=True)  37.6 us
    ppermute x5, waiting for transfers between devices, swap(): return lax.ppermute(value, 'bus', [(i, i ^ bits) for i in range(devices)])  29 us
    pallas_call x1, Pallas kernels, encode(): pl.pallas_call(encode_kernel, grid_spec=pltpu.PrefetchScalarGridSpec(num_...  22.3 us
    all_to_all x2, starting transfers between devices, exchange(): return lax.all_to_all(value, 'bus', split_axis=0, concat_axis=0, tiled=True)  11.8 us
    ppermute x5, starting transfers between devices, swap(): return lax.ppermute(value, 'bus', [(i, i ^ bits) for i in range(devices)])  5.21 us
    pallas_call x1, Pallas kernels, settle(): pl.pallas_call(settle_kernel, grid_spec=pltpu.PrefetchScalarGridSpec(num_...  5.12 us
  transfers between devices with their start and end apart: 7, of which 4 were waited for; matrix products, arithmetic and copies ran while one was open for 3% of the time, Pallas kernels for 39%

profile of v3, /device:TPU:12, one launch (start us, length us, event | category | flops | bytes accessed | tf_op | source)
XLA Modules:
  0.0 163.3 jit_solution(14384460244288410077)
XLA Ops:
  0.6 0.0 copy-start.12
  0.6 0.0 copy-start.11
  0.7 0.0 copy-start.13
  0.7 6.4 %all-to-all-start = ((bf16[16,128,512]{2,1,0:T(8,128)(2,1)}), bf16[16,128,512]{2,1,0:T(8,128)(2,1)S(1)}, u32[]{:S(2)}, u32[]{:S(2)}) async-start(bf16[16,128,512]{2,1,0:T(8,128)(2,1)} %param.21), calls=%async_computation | async-start | bytes 4194304 | tf_op jit(solution)/shard_map/all_to_all | solution.py:390
  7.7 0.0 copy-done.12
  7.7 0.7 copy.19.neighbors_ref
  8.4 0.0 copy-done.11
  8.4 1.4 copy.18.order_ref
  9.7 0.0 copy-done.13
  9.7 0.5 broadcast_multiply_fusion.scale_ref
  10.2 22.3 %encode.1 = (bf16[2048,512]{1,0:T(8,128)(2,1)}, bf16[2048,512]{1,0:T(8,128)(2,1)}, bf16[2048,512]{1,0:T(8,128)(2,1)}) custom-call(s32[1]{0:T(128)S(6)} %copy.39.hour_ref, s32[2048,1]{1,0:T(8,128)} %copy.18.order_ref, bf16[2048,1024]{1,0:T(8,128)(2,1)} %bitcast.80, bf16[24,1024]{1,0:T(8,128)(2,1)} %table_ref.1, f32[1,1024]{1,0:T(1,128)} %bitcast.81, ...), custom_call_target="tpu_custom_call" | custom-call | flops 15032385536 | bytes 13631488 | tf_op jit(solution)/shard_map/encode/pallas_call | solution.py:55
  32.5 16.7 %weights.1 = (bf16[4,16,384,256]{3,2,1,0:T(8,128)(2,1)}, bf16[4,16,128,256]{3,2,1,0:T(8,128)(2,1)}, f32[4,16,256]{2,1,0:T(8,128)}) custom-call(s32[16,3]{1,0:T(8,128)} %copy.19.neighbors_ref, f32[8]{0:T(128)} %broadcast_multiply_fusion.scale_ref, bf16[2048,512]{1,0:T(8,128)(2,1)} %get-tuple-element.14.q_ref, bf16[2048,512]{1,0:T(8,128)(2,1)} %get-tuple-element.15.k_ref, ...), custom_call_target="tpu_custom_call" | custom-call | flops 1610612736 | bytes 100663296 | tf_op jit(solution)/shard_map/weights/pallas_call | solution.py:346
  49.2 5.1 %all-to-all-done = bf16[16,128,512]{2,1,0:T(8,128)(2,1)S(1)} async-done(((bf16[16,128,512]{2,1,0:T(8,128)(2,1)}), bf16[16,128,512]{2,1,0:T(8,128)(2,1)S(1)}, u32[]{:S(2)}, u32[]{:S(2)}) %all-to-all-start) | async-done | bytes 2097184 | tf_op jit(solution)/shard_map/all_to_all | solution.py:390
  54.3 5.5 %value_early.1 = bf16[2048,256]{1,0:T(8,128)(2,1)} custom-call(s32[1]{0:T(128)} %bitcast.me_ref, bf16[4,16,384,256]{3,2,1,0:T(8,128)(2,1)} %get-tuple-element.17.refs_0_.w_ref, bf16[2048,512]{1,0:T(8,128)(2,1)S(1)} %bitcast.70), custom_call_target="tpu_custom_call" | custom-call | flops 402653184 | bytes 117440512 | tf_op jit(solution)/shard_map/value_early/pallas_call | solution.py:346
  59.8 1.3 fusion.12
  61.1 1.5 collective-permute-start.1
  62.6 0.0 collective-permute-start.2
  62.6 0.0 copy-start.4
  62.6 3.0 %collective-permute-start = (bf16[4,128,256]{2,1,0:T(8,128)(2,1)S(1)}, bf16[4,128,256]{2,1,0:T(8,128)(2,1)S(1)}, u32[]{:S(2)}, u32[]{:S(2)}) collective-permute-start(bf16[4,128,256]{2,1,0:T(8,128)(2,1)S(1)} %bitcast.76), channel_id=1, source_target_pairs={{0,4},{1,5},{2,6},{3,7},{4,0},{5,1},{6,2},{7,3},{8,12},{9,13},{10,... | collective-permute-start | bytes 786440 | tf_op jit(solution)/shard_map/ppermute | solution.py:277
  65.6 0.0 copy-done
  65.6 4.7 %value_late.1.rest_0_ = bf16[2048,768]{1,0:T(8,128)(2,1)} custom-call(bf16[4,16,384,256]{3,2,1,0:T(8,128)(2,1)} %get-tuple-element.17.refs_0_.w_ref, bf16[2048,512]{1,0:T(8,128)(2,1)S(1)} %bitcast.71), custom_call_target="tpu_custom_call" | custom-call | flops 402653184 | bytes 117440512 | tf_op jit(solution)/shard_map/value_late/pallas_call | solution.py:346
  70.4 0.0 copy-done.1
  70.4 0.0 copy-done.2
  70.4 14.7 %key.1 = bf16[2048,768]{1,0:T(8,128)(2,1)} custom-call(s32[16,3]{1,0:T(8,128)S(1)} %copy-done.3, f32[8]{0:T(128)S(1)} %copy-done.4, bf16[2048,512]{1,0:T(8,128)(2,1)S(1)} %copy-done.1, bf16[2048,512]{1,0:T(8,128)(2,1)} %get-tuple-element.15.k_ref, bf16[2048,512]{1,0:T(8,128)(2,1)} %get-tuple-element.16.v_ref, ...), custom_call_target="tpu_custom_call", output_to_operand_aliasing={{}: (8, {})} | custom-call | flops 2415919104 | bytes 252182528 | tf_op jit(solution)/shard_map/key/pallas_call | solution.py:346
  85.1 0.0 collective-permute-done.1
  85.1 0.0 collective-permute-done.2
  85.1 0.0 copy-start.5
  85.1 0.0 collective-permute-done
  85.1 0.7 copy-done.7
  85.8 0.1 copy-done.5
  85.8 0.1 copy-done.9
  85.9 5.4 %all-to-all-start.1 = ((bf16[16,128,768]{2,1,0:T(8,128)(2,1)}), bf16[16,128,768]{2,1,0:T(8,128)(2,1)S(1)}, u32[]{:S(2)}, u32[]{:S(2)}) async-start(bf16[16,128,768]{2,1,0:T(8,128)(2,1)} %bitcast.73), calls=%async_computation.1 | async-start | bytes 6291456 | tf_op jit(solution)/shard_map/all_to_all | solution.py:390
  91.4 0.0 slice-start.1
  91.4 0.0 slice-start.2
  91.4 1.0 slice_bitcast_fusion.2
  92.4 1.0 slice_bitcast_fusion
  93.3 0.0 copy-start.10
  93.4 0.1 pad_maximum_fusion
  93.4 0.0 copy-start.8
  93.4 0.0 copy-start.6
  93.5 0.6 collective-permute-start.3
  94.2 27.1 %collective-permute-done.3 = bf16[4,2,128,256]{3,2,1,0:T(8,128)(2,1)S(1)} collective-permute-done((bf16[4,2,128,256]{3,2,1,0:T(8,128)(2,1)S(1)}, bf16[4,2,128,256]{3,2,1,0:T(8,128)(2,1)S(1)}, u32[]{:S(2)}, u32[]{:S(2)}) %collective-permute-start.3) | collective-permute-done | bytes 524320 | tf_op jit(solution)/shard_map/ppermute | solution.py:277
  121.3 0.1 pad_maximum_fusion.1
  121.3 0.1 collective-permute-start.4
  121.4 1.9 %collective-permute-done.4 = bf16[4,2,128,256]{3,2,1,0:T(8,128)(2,1)S(1)} collective-permute-done((bf16[4,2,128,256]{3,2,1,0:T(8,128)(2,1)S(1)}, bf16[4,2,128,256]{3,2,1,0:T(8,128)(2,1)S(1)}, u32[]{:S(2)}, u32[]{:S(2)}) %collective-permute-start.4) | collective-permute-done | bytes 524320 | tf_op jit(solution)/shard_map/ppermute | solution.py:277
  123.5 5.1 %settle.1._ = bf16[16,128,512]{2,1,0:T(8,128)(2,1)} custom-call(s32[1]{0:T(128)} %bitcast.me_ref, bf16[16,128,256]{2,1,0:T(8,128)(2,1)S(1)} %fusion.x_ref), custom_call_target="tpu_custom_call" | custom-call | bytes 2097152 | tf_op jit(solution)/shard_map/settle/pallas_call | solution.py:260
  128.7 32.5 %all-to-all-done.1.late_ref = bf16[16,128,768]{2,1,0:T(8,128)(2,1)S(1)} async-done(((bf16[16,128,768]{2,1,0:T(8,128)(2,1)}), bf16[16,128,768]{2,1,0:T(8,128)(2,1)S(1)}, u32[]{:S(2)}, u32[]{:S(2)}) %all-to-all-start.1) | async-done | bytes 3145760 | tf_op jit(solution)/shard_map/all_to_all | solution.py:390
  161.1 2.1 %part.1 = (bf16[16,128,512]{2,1,0:T(8,128)(2,1)}, bf16[16,128,512]{2,1,0:T(8,128)(2,1)}) custom-call(bf16[16,128,768]{2,1,0:T(8,128)(2,1)S(1)} %all-to-all-done.1.late_ref, bf16[16,128,512]{2,1,0:T(8,128)(2,1)} %settle.1._), custom_call_target="tpu_custom_call", output_to_operand_aliasing={{1}: (1, {})} | custom-call | bytes 6291456 | tf_op jit(solution)/shard_map/part/pallas_call | solution.py:312
  (33 shorter events, 0.2 us)
Async XLA Ops:
  0.6 7.1 %copy-start.12 = (s32[16,3]{0,1:T(4,128)S(1)}, s32[16,3]{0,1:T(4,128)}, u32[]{:S(2)}) copy-start(s32[16,3]{0,1:T(4,128)} %param.20) | copy-start | bytes 580
  0.6 7.7 %copy-start.11 = (s32[2048]{0:T(1024)S(1)}, s32[2048]{0:T(1024)}, u32[]{:S(2)}) copy-start(s32[2048]{0:T(1024)} %param.15) | copy-start | bytes 24580
  0.7 9.1 %copy-start.13 = (f32[8]{0:T(128)S(1)}, f32[8]{0:T(128)}, u32[]{:S(2)}) copy-start(f32[8]{0:T(128)} %param.19) | copy-start | bytes 100
  0.7 53.7 %all-to-all-start = ((bf16[16,128,512]{2,1,0:T(8,128)(2,1)}), bf16[16,128,512]{2,1,0:T(8,128)(2,1)S(1)}, u32[]{:S(2)}, u32[]{:S(2)}) async-start(bf16[16,128,512]{2,1,0:T(8,128)(2,1)} %param.21), calls=%async_computation | async-start | bytes 4194304 | tf_op jit(solution)/shard_map/all_to_all | solution.py:390
  54.3 11.3 %copy-start = (bf16[16,128,512]{2,1,0:T(8,128)(2,1)}, bf16[16,128,512]{2,1,0:T(8,128)(2,1)S(1)}, u32[]{:S(2)}) copy-start(bf16[16,128,512]{2,1,0:T(8,128)(2,1)S(1)} %all-to-all-done) | copy-start | bytes 6291460
  61.1 24.0 %collective-permute-start.1 = (bf16[4,128,256]{2,1,0:T(8,128)(2,1)S(1)}, bf16[4,128,256]{2,1,0:T(8,128)(2,1)S(1)}, u32[]{:S(2)}, u32[]{:S(2)}) collective-permute-start(bf16[4,128,256]{2,1,0:T(8,128)(2,1)S(1)} %bitcast.78), channel_id=1, source_target_pairs={{0,8},{1,9},{2,10},{3,11},{4,12},{5,13},{6,14},{7,15},{8,0},{9,1},... | collective-permute-start | bytes 786440 | tf_op jit(solution)/shard_map/ppermute | solution.py:277
  62.6 22.5 %collective-permute-start.2 = (bf16[4,128,256]{2,1,0:T(8,128)(2,1)S(1)}, bf16[4,128,256]{2,1,0:T(8,128)(2,1)S(1)}, u32[]{:S(2)}, u32[]{:S(2)}) collective-permute-start(bf16[4,128,256]{2,1,0:T(8,128)(2,1)S(1)} %bitcast.77), channel_id=1, source_target_pairs={{0,12},{1,13},{2,14},{3,15},{4,8},{5,9},{6,10},{7,11},{8,4},{9,5},... | collective-permute-start | bytes 786440 | tf_op jit(solution)/shard_map/ppermute | solution.py:277
  62.6 7.8 %copy-start.1 = (bf16[2048,512]{1,0:T(8,128)(2,1)S(1)}, bf16[2048,512]{1,0:T(8,128)(2,1)}, u32[]{:S(2)}) copy-start(bf16[2048,512]{1,0:T(8,128)(2,1)} %get-tuple-element.14.q_ref) | copy-start | bytes 6291460
  62.6 7.8 %copy-start.2 = (f32[4,16,256]{2,1,0:T(8,128)S(1)}, f32[4,16,256]{2,1,0:T(8,128)}, u32[]{:S(2)}) copy-start(f32[4,16,256]{2,1,0:T(8,128)} %get-tuple-element.20.shift_ref) | copy-start | bytes 196612
  62.6 7.8 %copy-start.3 = (s32[16,3]{1,0:T(8,128)S(1)}, s32[16,3]{1,0:T(8,128)}, u32[]{:S(2)}) copy-start(s32[16,3]{1,0:T(8,128)} %copy.19.neighbors_ref) | copy-start | bytes 580
  62.6 7.8 %copy-start.4 = (f32[8]{0:T(128)S(1)}, f32[8]{0:T(128)}, u32[]{:S(2)}) copy-start(f32[8]{0:T(128)} %broadcast_multiply_fusion.scale_ref) | copy-start | bytes 100
  62.6 22.5 %collective-permute-start = (bf16[4,128,256]{2,1,0:T(8,128)(2,1)S(1)}, bf16[4,128,256]{2,1,0:T(8,128)(2,1)S(1)}, u32[]{:S(2)}, u32[]{:S(2)}) collective-permute-start(bf16[4,128,256]{2,1,0:T(8,128)(2,1)S(1)} %bitcast.76), channel_id=1, source_target_pairs={{0,4},{1,5},{2,6},{3,7},{4,0},{5,1},{6,2},{7,3},{8,12},{9,13},{10,... | collective-permute-start | bytes 786440 | tf_op jit(solution)/shard_map/ppermute | solution.py:277
  85.1 0.7 copy-start.7
  85.1 0.8 copy-start.5
  85.1 0.8 copy-start.9
  85.9 75.2 %all-to-all-start.1 = ((bf16[16,128,768]{2,1,0:T(8,128)(2,1)}), bf16[16,128,768]{2,1,0:T(8,128)(2,1)S(1)}, u32[]{:S(2)}, u32[]{:S(2)}) async-start(bf16[16,128,768]{2,1,0:T(8,128)(2,1)} %bitcast.73), calls=%async_computation.1 | async-start | bytes 6291456 | tf_op jit(solution)/shard_map/all_to_all | solution.py:390
  91.4 2.8 %slice-start = ((bf16[4,128,256]{2,1,0:T(8,128)(2,1)}), bf16[1,128,256]{2,1,0:T(8,128)(2,1)S(1)}, s32[]{:S(2)}) async-start(bf16[4,128,256]{2,1,0:T(8,128)(2,1)} %copy-done.5), calls=%async_computation.2 | async-start | bytes 131072 | tf_op jit(solution)/shard_map/slice | solution.py:292
  91.4 2.8 %slice-start.1 = ((bf16[4,128,256]{2,1,0:T(8,128)(2,1)}), bf16[1,128,256]{2,1,0:T(8,128)(2,1)S(1)}, s32[]{:S(2)}) async-start(bf16[4,128,256]{2,1,0:T(8,128)(2,1)} %copy-done.7), calls=%async_computation.3 | async-start | bytes 131072 | tf_op jit(solution)/shard_map/slice | solution.py:292
  91.4 2.8 %slice-start.2 = ((bf16[4,128,256]{2,1,0:T(8,128)(2,1)}), bf16[1,128,256]{2,1,0:T(8,128)(2,1)S(1)}, s32[]{:S(2)}) async-start(bf16[4,128,256]{2,1,0:T(8,128)(2,1)} %copy-done.9), calls=%async_computation.4 | async-start | bytes 131072 | tf_op jit(solution)/shard_map/slice | solution.py:292
  93.3 30.0 %copy-start.10 = (bf16[4,128,256]{2,1,0:T(8,128)(2,1)S(1)}, bf16[4,128,256]{2,1,0:T(8,128)(2,1)}, u32[]{:S(2)}) copy-start(bf16[4,128,256]{2,1,0:T(8,128)(2,1)} %copy-done.9) | copy-start | bytes 786436
  93.4 30.0 %copy-start.8 = (bf16[4,128,256]{2,1,0:T(8,128)(2,1)S(1)}, bf16[4,128,256]{2,1,0:T(8,128)(2,1)}, u32[]{:S(2)}) copy-start(bf16[4,128,256]{2,1,0:T(8,128)(2,1)} %copy-done.7) | copy-start | bytes 786436
  93.4 30.0 %copy-start.6 = (bf16[4,128,256]{2,1,0:T(8,128)(2,1)S(1)}, bf16[4,128,256]{2,1,0:T(8,128)(2,1)}, u32[]{:S(2)}) copy-start(bf16[4,128,256]{2,1,0:T(8,128)(2,1)} %copy-done.5) | copy-start | bytes 786436
  93.5 27.8 %collective-permute-start.3 = (bf16[4,2,128,256]{3,2,1,0:T(8,128)(2,1)S(1)}, bf16[4,2,128,256]{3,2,1,0:T(8,128)(2,1)S(1)}, u32[]{:S(2)}, u32[]{:S(2)}) collective-permute-start(bf16[4,2,128,256]{3,2,1,0:T(8,128)(2,1)S(1)} %pad_maximum_fusion), channel_id=1, source_target_pairs={{0,2},{1,3},{2,0},{3,1},{4,6},{5,7},{6,4},{7,5},{8,10},{9,11},{10,... | collective-permute-start | bytes 1572872 | tf_op jit(solution)/shard_map/ppermute | solution.py:277
  121.3 2.0 %collective-permute-start.4 = (bf16[4,2,128,256]{3,2,1,0:T(8,128)(2,1)S(1)}, bf16[4,2,128,256]{3,2,1,0:T(8,128)(2,1)S(1)}, u32[]{:S(2)}, u32[]{:S(2)}) collective-permute-start(bf16[4,2,128,256]{3,2,1,0:T(8,128)(2,1)S(1)} %pad_maximum_fusion.1), channel_id=1, source_target_pairs={{0,1},{1,0},{2,3},{3,2},{4,5},{5,4},{6,7},{7,6},{8,9},{9,8},{10,11... | collective-permute-start | bytes 1572872 | tf_op jit(solution)/shard_map/ppermute | solution.py:277

commit v4 on v3

--- a/solution.py
+++ b/solution.py
@@ -11,7 +11,7 @@
 EPSILON = 1e-05
 NEG_FILL = -1e30
 VMEM_LIMIT = 56 << 20
-SETTLE_STEPS = 4
+SETTLE_STEPS = 2
 EARLY_PAIRS = 2
 PLANE = 4
 
@@ -131,14 +131,11 @@
 
 
 class KeySums:
-    def __init__(self, out_ref, rows, flip=None):
-        self.out_ref, self.rows, self.flip, self.open = out_ref, rows, flip, [None, None]
+    def __init__(self, out_ref, rows):
+        self.out_ref, self.rows, self.open = out_ref, rows, [None, None]
 
     def store(self, block, value):
-        start = block * self.rows
-        if self.flip is not None:
-            start = pl.multiple_of((self.flip ^ block) * self.rows, self.rows)
-        self.out_ref[pl.ds(start, self.rows), :] = value.astype(jnp.bfloat16)
+        self.out_ref[block * self.rows : (block + 1) * self.rows, :] = value.astype(jnp.bfloat16)
 
     def add(self, block, part):
         low, own, high = [part[d * self.rows : (d + 1) * self.rows] for d in range(3)]
@@ -177,14 +174,20 @@
     attend(blocks - 1, last)
 
 
-def flipped_value_kernel(rows, me_ref, *refs):
-    value_kernel(rows, *refs, flip=me_ref[0])
-
-
-def value_kernel(rows, w_ref, g_ref, *rest, flip=None):
+def early_value_kernel(rows, me_ref, w_ref, g_ref, *rest):
+    *outs, held = rest
+    value_kernel(rows, w_ref, g_ref, held)
+    for k, out in enumerate(outs):
+        for i in range(PLANE):
+            block = me_ref[0] ^ (PLANE * k + i)
+            tile = held[pl.ds(pl.multiple_of(block * rows, rows), rows), :]
+            out[i * rows : (i + 1) * rows, :] = tile
+
+
+def value_kernel(rows, w_ref, g_ref, *rest):
     dv_ref = rest[-1]
     blocks = g_ref.shape[0] // rows
-    sums = KeySums(dv_ref, rows, flip)
+    sums = KeySums(dv_ref, rows)
 
     def products(b):
         g_two = both_heads(tile_at(g_ref, b, rows))
@@ -278,12 +281,7 @@
 
 
 def swap_far(parts):
-    devices = parts.shape[0]
-    planes = devices // PLANE
-
-    far = [parts[:PLANE]]
-    far += [swap(parts[PLANE * k : PLANE * (k + 1)], PLANE * k) for k in range(1, planes)]
-    return far
+    return [parts[0]] + [swap(part, PLANE * k) for k, part in enumerate(parts) if k]
 
 
 def swap_near(far):
@@ -327,7 +325,7 @@
 
 def by_pair(
     kernel, name, rows, heads, feat, first, count, scalars, arrays, outs, out_first, dots, exps,
-    into=None, limit=50,
+    into=None, limit=50, scratch=(),
 ):
     buses, lanes = arrays[1].shape[0], 2 * feat // heads
 
@@ -335,7 +333,7 @@
         if len(shape) > 2:
             zeros = (0,) * (len(shape) - 1)
             return pl.BlockSpec((1,) + shape[1:], lambda p, *_: (at + p, *zeros))
-        return pl.BlockSpec((buses, lanes), lambda p, *_: (0, at + p))
+        return pl.BlockSpec((shape[0], lanes), lambda p, *_: (0, at + p))
 
     specs = [spec(x.shape, first) for x in arrays]
     arrays, alias = list(arrays), {}
@@ -350,6 +348,7 @@
             grid=(count,),
             in_specs=specs,
             out_specs=[spec(x.shape, out_first) for x in outs],
+            scratch_shapes=scratch,
         ),
         out_shape=[pltpu.HBM(x.shape, x.dtype) for x in outs],
         input_output_aliases=alias,
@@ -411,12 +410,15 @@
             jax.ShapeDtypeStruct((pairs, bus_blocks, 2 * block_rows), jnp.float32),
         ],
     )
-    (early_value,) = call(
-        flipped_value_kernel, "value_early", first=0, count=early, scalars=(me,),
-        arrays=(weights, grads), outs=[bf16(bus_count, early * lanes)], out_first=0,
-        dots=1, exps=0,
-    )
-    early_far = swap_far(blocks_of(early_value))
+    early_value = call(
+        early_value_kernel, "value_early", first=0, count=early, scalars=(me,),
+        arrays=(weights, grads), out_first=0, dots=1, exps=0,
+        outs=[bf16(PLANE * block_rows, early * lanes)] * (devices // PLANE),
+        scratch=[pltpu.VMEM((bus_count, lanes), jnp.bfloat16)],
+    )
+    early_far = swap_far(
+        [x.reshape(PLANE, block_rows, early * lanes) for x in early_value]
+    )
     grads, _ = lax.optimization_barrier((grads, early_value))
     rest_out = bf16(bus_count, late * lanes + feat_width)
     (rest,) = call(

time: 164 us -> 163 us (level)
  waiting for transfers between devices: 66.6 us -> 61.7 us
  local copies, waits for them, and re-layouts: 6.26 us -> 8.78 us
    ppermute x5, waiting for transfers between devices: 29 us -> 25.7 us  [swap(): return lax.ppermute(value, 'bus', [(i, i ^ bits) for i in range(devices)])]
    slice x7 -> x4, local copies, waits for them, and re-layouts: 0.02 us -> 2.96 us  [swap_near(): entry[1]]
    all_to_all x2, waiting for transfers between devices: 37.6 us -> 35.9 us  [exchange(): return lax.all_to_all(value, 'bus', split_axis=0, concat_axis=0, tiled=True)]
  transfers between devices with their start and end apart: 7 -> 7, of which waited for: 4 -> 5; matrix products, arithmetic and copies ran while one was open for 3% -> 6% of each run, Pallas kernels for 39% -> 39%
where the time goes in v4:
time: 163 us; the launch traced here: 162 us
  Pallas kernels  70.7 us (43%)
  waiting for transfers between devices  61.7 us (38%)
  starting transfers between devices  17.7 us (11%)
  local copies, waits for them, and re-layouts  8.78 us (5%)
    pallas_call x4, Pallas kernels, by_pair(): pl.pallas_call(functools.partial(kernel, rows), grid_spec=pltpu.PrefetchS...  41.6 us
    all_to_all x2, waiting for transfers between devices, exchange(): return lax.all_to_all(value, 'bus', split_axis=0, concat_axis=0, tiled=True)  35.9 us
    ppermute x5, waiting for transfers between devices, swap(): return lax.ppermute(value, 'bus', [(i, i ^ bits) for i in range(devices)])  25.7 us
    pallas_call x1, Pallas kernels, encode(): pl.pallas_call(encode_kernel, grid_spec=pltpu.PrefetchScalarGridSpec(num_...  22.2 us
    all_to_all x2, starting transfers between devices, exchange(): return lax.all_to_all(value, 'bus', split_axis=0, concat_axis=0, tiled=True)  13.4 us
    pallas_call x1, Pallas kernels, settle(): pl.pallas_call(settle_kernel, grid_spec=pltpu.PrefetchScalarGridSpec(num_...  5.12 us
    ppermute x5, starting transfers between devices, swap(): return lax.ppermute(value, 'bus', [(i, i ^ bits) for i in range(devices)])  4.25 us
  transfers between devices with their start and end apart: 7, of which 5 were waited for; matrix products, arithmetic and copies ran while one was open for 6% of the time, Pallas kernels for 39%

profile of v4, /device:TPU:12, one launch (start us, length us, event | category | flops | bytes accessed | tf_op | source)
XLA Modules:
  0.0 161.9 jit_solution(12978505197547308257)
XLA Ops:
  0.6 0.0 copy-start.7
  0.6 0.0 copy-start.6
  0.7 0.0 copy-start.8
  0.7 6.4 %all-to-all-start = ((bf16[16,128,512]{2,1,0:T(8,128)(2,1)}), bf16[16,128,512]{2,1,0:T(8,128)(2,1)S(1)}, u32[]{:S(2)}, u32[]{:S(2)}) async-start(bf16[16,128,512]{2,1,0:T(8,128)(2,1)} %param.21), calls=%async_computation | async-start | bytes 4194304 | tf_op jit(solution)/shard_map/all_to_all | solution.py:389
  7.7 0.0 copy-done.7
  7.7 0.7 copy.19.neighbors_ref
  8.4 0.0 copy-done.6
  8.4 1.4 copy.18.order_ref
  9.8 0.0 copy-done.8
  9.8 0.6 broadcast_multiply_fusion.scale_ref
  10.3 22.2 %encode.1 = (bf16[2048,512]{1,0:T(8,128)(2,1)}, bf16[2048,512]{1,0:T(8,128)(2,1)}, bf16[2048,512]{1,0:T(8,128)(2,1)}) custom-call(s32[1]{0:T(128)S(6)} %copy.39.hour_ref, s32[2048,1]{1,0:T(8,128)} %copy.18.order_ref, bf16[2048,1024]{1,0:T(8,128)(2,1)} %bitcast.77, bf16[24,1024]{1,0:T(8,128)(2,1)} %table_ref.1, f32[1,1024]{1,0:T(1,128)} %bitcast.81, ...), custom_call_target="tpu_custom_call" | custom-call | flops 15032385536 | bytes 13631488 | tf_op jit(solution)/shard_map/encode/pallas_call | solution.py:55
  32.6 16.7 %weights.1 = (bf16[4,16,384,256]{3,2,1,0:T(8,128)(2,1)}, bf16[4,16,128,256]{3,2,1,0:T(8,128)(2,1)}, f32[4,16,256]{2,1,0:T(8,128)}) custom-call(s32[16,3]{1,0:T(8,128)} %copy.19.neighbors_ref, f32[8]{0:T(128)} %broadcast_multiply_fusion.scale_ref, bf16[2048,512]{1,0:T(8,128)(2,1)} %get-tuple-element.18.q_ref, bf16[2048,512]{1,0:T(8,128)(2,1)} %get-tuple-element.19.k_ref, ...), custom_call_target="tpu_custom_call" | custom-call | flops 1610612736 | bytes 100663296 | tf_op jit(solution)/shard_map/weights/pallas_call | solution.py:344
  49.2 5.1 %all-to-all-done = bf16[16,128,512]{2,1,0:T(8,128)(2,1)S(1)} async-done(((bf16[16,128,512]{2,1,0:T(8,128)(2,1)}), bf16[16,128,512]{2,1,0:T(8,128)(2,1)S(1)}, u32[]{:S(2)}, u32[]{:S(2)}) %all-to-all-start) | async-done | bytes 2097184 | tf_op jit(solution)/shard_map/all_to_all | solution.py:389
  54.3 0.0 copy-start
  54.3 5.5 %value_early.1 = (bf16[512,256]{1,0:T(8,128)(2,1)}, bf16[512,256]{1,0:T(8,128)(2,1)}, bf16[512,256]{1,0:T(8,128)(2,1)}, bf16[512,256]{1,0:T(8,128)(2,1)}) custom-call(s32[1]{0:T(128)} %bitcast.me_ref, bf16[4,16,384,256]{3,2,1,0:T(8,128)(2,1)} %get-tuple-element.21.w_ref, bf16[2048,512]{1,0:T(8,128)(2,1)S(1)} %bitcast.70), custom_call_target="tpu_custom_call" | custom-call | flops 402653184 | bytes 117440512 | tf_op jit(solution)/shard_map/value_early/pallas_call | solution.py:344
  59.8 0.1 collective-permute-start.2
  60.0 1.3 collective-permute-start.1
  61.3 0.0 copy-start.1
  61.3 0.0 copy-start.2
  61.3 2.1 %collective-permute-start = (bf16[4,128,256]{2,1,0:T(8,128)(2,1)}, bf16[4,128,256]{2,1,0:T(8,128)(2,1)}, u32[]{:S(2)}, u32[]{:S(2)}) collective-permute-start(bf16[4,128,256]{2,1,0:T(8,128)(2,1)} %bitcast.78), channel_id=1, source_target_pairs={{0,4},{1,5},{2,6},{3,7},{4,0},{5,1},{6,2},{7,3},{8,12},{9,13},{10,... | collective-permute-start | bytes 786440 | tf_op jit(solution)/shard_map/ppermute | solution.py:280
  63.4 0.0 copy-done
  63.4 4.7 %value_late.1.rest_0_ = bf16[2048,768]{1,0:T(8,128)(2,1)} custom-call(bf16[4,16,384,256]{3,2,1,0:T(8,128)(2,1)} %get-tuple-element.21.w_ref, bf16[2048,512]{1,0:T(8,128)(2,1)S(1)} %bitcast.71), custom_call_target="tpu_custom_call" | custom-call | flops 402653184 | bytes 117440512 | tf_op jit(solution)/shard_map/value_late/pallas_call | solution.py:344
  68.2 0.0 copy-done.1
  68.2 0.0 copy-done.2
  68.2 0.0 copy-done.3
  68.2 0.0 copy-done.4
  68.2 14.7 %key.1 = bf16[2048,768]{1,0:T(8,128)(2,1)} custom-call(s32[16,3]{1,0:T(8,128)S(1)} %copy-done.3, f32[8]{0:T(128)S(1)} %copy-done.4, bf16[2048,512]{1,0:T(8,128)(2,1)S(1)} %copy-done.1, bf16[2048,512]{1,0:T(8,128)(2,1)} %get-tuple-element.19.k_ref, bf16[2048,512]{1,0:T(8,128)(2,1)} %get-tuple-element.20.v_ref, ...), custom_call_target="tpu_custom_call", output_to_operand_aliasing={{}: (8, {})} | custom-call | flops 2415919104 | bytes 252182528 | tf_op jit(solution)/shard_map/key/pallas_call | solution.py:344
  82.8 0.0 collective-permute-done.2
  82.8 0.5 collective-permute-done.1
  83.3 0.0 collective-permute-done
  83.3 7.0 %all-to-all-start.1 = ((bf16[16,128,768]{2,1,0:T(8,128)(2,1)}), bf16[16,128,768]{2,1,0:T(8,128)(2,1)S(1)}, u32[]{:S(2)}, u32[]{:S(2)}) async-start(bf16[16,128,768]{2,1,0:T(8,128)(2,1)} %bitcast.73), calls=%async_computation.1 | async-start | bytes 6291456 | tf_op jit(solution)/shard_map/all_to_all | solution.py:389
  90.4 1.0 slice_bitcast_fusion.2
  91.4 0.9 slice_bitcast_fusion
  92.3 0.1 pad_maximum_fusion
  92.4 0.6 collective-permute-start.3
  93.0 1.5 slice.77
  94.5 1.5 slice.78
  96.0 0.0 copy-done.5
  96.0 0.9 maximum_bitcast_fusion
  96.9 23.3 %collective-permute-done.3 = bf16[4,2,128,256]{3,2,1,0:T(8,128)(2,1)S(1)} collective-permute-done((bf16[4,2,128,256]{3,2,1,0:T(8,128)(2,1)S(1)}, bf16[4,2,128,256]{3,2,1,0:T(8,128)(2,1)S(1)}, u32[]{:S(2)}, u32[]{:S(2)}) %collective-permute-start.3) | collective-permute-done | bytes 524320 | tf_op jit(solution)/shard_map/ppermute | solution.py:280
  120.3 0.1 pad_maximum_fusion.1
  120.3 0.1 collective-permute-start.4
  120.4 1.9 %collective-permute-done.4 = bf16[4,2,128,256]{3,2,1,0:T(8,128)(2,1)S(1)} collective-permute-done((bf16[4,2,128,256]{3,2,1,0:T(8,128)(2,1)S(1)}, bf16[4,2,128,256]{3,2,1,0:T(8,128)(2,1)S(1)}, u32[]{:S(2)}, u32[]{:S(2)}) %collective-permute-start.4) | collective-permute-done | bytes 524320 | tf_op jit(solution)/shard_map/ppermute | solution.py:280
  122.3 0.8 slice_dynamic-update-slice_fusion.2
  123.2 0.8 slice_dynamic-update-slice_fusion.1
  124.2 5.1 %settle.1._ = bf16[16,128,512]{2,1,0:T(8,128)(2,1)} custom-call(s32[1]{0:T(128)} %bitcast.me_ref, bf16[16,128,256]{2,1,0:T(8,128)(2,1)S(1)} %fusion.x_ref), custom_call_target="tpu_custom_call" | custom-call | bytes 2097152 | tf_op jit(solution)/shard_map/settle/pallas_call | solution.py:263
  129.3 30.9 %all-to-all-done.1.late_ref = bf16[16,128,768]{2,1,0:T(8,128)(2,1)S(1)} async-done(((bf16[16,128,768]{2,1,0:T(8,128)(2,1)}), bf16[16,128,768]{2,1,0:T(8,128)(2,1)S(1)}, u32[]{:S(2)}, u32[]{:S(2)}) %all-to-all-start.1) | async-done | bytes 3145760 | tf_op jit(solution)/shard_map/all_to_all | solution.py:389
  160.1 1.8 %part.1 = (bf16[16,128,512]{2,1,0:T(8,128)(2,1)}, bf16[16,128,512]{2,1,0:T(8,128)(2,1)}) custom-call(bf16[16,128,768]{2,1,0:T(8,128)(2,1)S(1)} %all-to-all-done.1.late_ref, bf16[16,128,512]{2,1,0:T(8,128)(2,1)} %settle.1._), custom_call_target="tpu_custom_call", output_to_operand_aliasing={{1}: (1, {})} | custom-call | bytes 6291456 | tf_op jit(solution)/shard_map/part/pallas_call | solution.py:310
  (19 shorter events, 0.1 us)
Async XLA Ops:
  0.6 7.1 %copy-start.7 = (s32[16,3]{0,1:T(4,128)S(1)}, s32[16,3]{0,1:T(4,128)}, u32[]{:S(2)}) copy-start(s32[16,3]{0,1:T(4,128)} %param.20) | copy-start | bytes 580
  0.6 7.7 %copy-start.6 = (s32[2048]{0:T(1024)S(1)}, s32[2048]{0:T(1024)}, u32[]{:S(2)}) copy-start(s32[2048]{0:T(1024)} %param.15) | copy-start | bytes 24580
  0.7 9.1 %copy-start.8 = (f32[8]{0:T(128)S(1)}, f32[8]{0:T(128)}, u32[]{:S(2)}) copy-start(f32[8]{0:T(128)} %param.19) | copy-start | bytes 100
  0.7 53.7 %all-to-all-start = ((bf16[16,128,512]{2,1,0:T(8,128)(2,1)}), bf16[16,128,512]{2,1,0:T(8,128)(2,1)S(1)}, u32[]{:S(2)}, u32[]{:S(2)}) async-start(bf16[16,128,512]{2,1,0:T(8,128)(2,1)} %param.21), calls=%async_computation | async-start | bytes 4194304 | tf_op jit(solution)/shard_map/all_to_all | solution.py:389
  54.3 9.1 %copy-start = (bf16[16,128,512]{2,1,0:T(8,128)(2,1)}, bf16[16,128,512]{2,1,0:T(8,128)(2,1)S(1)}, u32[]{:S(2)}) copy-start(bf16[16,128,512]{2,1,0:T(8,128)(2,1)S(1)} %all-to-all-done) | copy-start | bytes 6291460
  59.8 23.0 %collective-permute-start.2 = (bf16[4,128,256]{2,1,0:T(8,128)(2,1)}, bf16[4,128,256]{2,1,0:T(8,128)(2,1)S(1)}, u32[]{:S(2)}, u32[]{:S(2)}) collective-permute-start(bf16[4,128,256]{2,1,0:T(8,128)(2,1)} %bitcast.80), channel_id=1, source_target_pairs={{0,12},{1,13},{2,14},{3,15},{4,8},{5,9},{6,10},{7,11},{8,4},{9,5},... | collective-permute-start | bytes 786440 | tf_op jit(solution)/shard_map/ppermute | solution.py:280
  60.0 23.4 %collective-permute-start.1 = (bf16[4,128,256]{2,1,0:T(8,128)(2,1)}, bf16[4,128,256]{2,1,0:T(8,128)(2,1)}, u32[]{:S(2)}, u32[]{:S(2)}) collective-permute-start(bf16[4,128,256]{2,1,0:T(8,128)(2,1)} %bitcast.79), channel_id=1, source_target_pairs={{0,8},{1,9},{2,10},{3,11},{4,12},{5,13},{6,14},{7,15},{8,0},{9,1},... | collective-permute-start | bytes 786440 | tf_op jit(solution)/shard_map/ppermute | solution.py:280
  61.3 6.9 %copy-start.1 = (bf16[2048,512]{1,0:T(8,128)(2,1)S(1)}, bf16[2048,512]{1,0:T(8,128)(2,1)}, u32[]{:S(2)}) copy-start(bf16[2048,512]{1,0:T(8,128)(2,1)} %get-tuple-element.18.q_ref) | copy-start | bytes 6291460
  61.3 6.9 %copy-start.2 = (f32[4,16,256]{2,1,0:T(8,128)S(1)}, f32[4,16,256]{2,1,0:T(8,128)}, u32[]{:S(2)}) copy-start(f32[4,16,256]{2,1,0:T(8,128)} %get-tuple-element.28.shift_ref) | copy-start | bytes 196612
  61.3 6.9 %copy-start.3 = (s32[16,3]{1,0:T(8,128)S(1)}, s32[16,3]{1,0:T(8,128)}, u32[]{:S(2)}) copy-start(s32[16,3]{1,0:T(8,128)} %copy.19.neighbors_ref) | copy-start | bytes 580
  61.3 6.9 %copy-start.4 = (f32[8]{0:T(128)S(1)}, f32[8]{0:T(128)}, u32[]{:S(2)}) copy-start(f32[8]{0:T(128)} %broadcast_multiply_fusion.scale_ref) | copy-start | bytes 100
  61.3 22.0 %collective-permute-start = (bf16[4,128,256]{2,1,0:T(8,128)(2,1)}, bf16[4,128,256]{2,1,0:T(8,128)(2,1)}, u32[]{:S(2)}, u32[]{:S(2)}) collective-permute-start(bf16[4,128,256]{2,1,0:T(8,128)(2,1)} %bitcast.78), channel_id=1, source_target_pairs={{0,4},{1,5},{2,6},{3,7},{4,0},{5,1},{6,2},{7,3},{8,12},{9,13},{10,... | collective-permute-start | bytes 786440 | tf_op jit(solution)/shard_map/ppermute | solution.py:280
  83.3 76.8 %all-to-all-start.1 = ((bf16[16,128,768]{2,1,0:T(8,128)(2,1)}), bf16[16,128,768]{2,1,0:T(8,128)(2,1)S(1)}, u32[]{:S(2)}, u32[]{:S(2)}) async-start(bf16[16,128,768]{2,1,0:T(8,128)(2,1)} %bitcast.73), calls=%async_computation.1 | async-start | bytes 6291456 | tf_op jit(solution)/shard_map/all_to_all | solution.py:389
  90.4 5.6 %copy-start.5 = (bf16[512,256]{1,0:T(8,128)(2,1)S(1)}, bf16[512,256]{1,0:T(8,128)(2,1)}, u32[]{:S(2)}) copy-start(bf16[512,256]{1,0:T(8,128)(2,1)} %get-tuple-element.22) | copy-start | bytes 786436
  92.4 27.9 %collective-permute-start.3 = (bf16[4,2,128,256]{3,2,1,0:T(8,128)(2,1)S(1)}, bf16[4,2,128,256]{3,2,1,0:T(8,128)(2,1)S(1)}, u32[]{:S(2)}, u32[]{:S(2)}) collective-permute-start(bf16[4,2,128,256]{3,2,1,0:T(8,128)(2,1)S(1)} %pad_maximum_fusion), channel_id=1, source_target_pairs={{0,2},{1,3},{2,0},{3,1},{4,6},{5,7},{6,4},{7,5},{8,10},{9,11},{10,... | collective-permute-start | bytes 1572872 | tf_op jit(solution)/shard_map/ppermute | solution.py:280
  120.3 2.0 %collective-permute-start.4 = (bf16[4,2,128,256]{3,2,1,0:T(8,128)(2,1)S(1)}, bf16[4,2,128,256]{3,2,1,0:T(8,128)(2,1)S(1)}, u32[]{:S(2)}, u32[]{:S(2)}) collective-permute-start(bf16[4,2,128,256]{3,2,1,0:T(8,128)(2,1)S(1)} %pad_maximum_fusion.1), channel_id=1, source_target_pairs={{0,1},{1,0},{2,3},{3,2},{4,5},{5,4},{6,7},{7,6},{8,9},{9,8},{10,11... | collective-permute-start | bytes 1572872 | tf_op jit(solution)/shard_map/ppermute | solution.py:280

commit v5 on v4

--- a/solution.py
+++ b/solution.py
@@ -325,7 +325,7 @@
 
 def by_pair(
     kernel, name, rows, heads, feat, first, count, scalars, arrays, outs, out_first, dots, exps,
-    into=None, limit=50, scratch=(),
+    into=None, limit=40, scratch=(),
 ):
     buses, lanes = arrays[1].shape[0], 2 * feat // heads
 
@@ -402,7 +402,7 @@
         w_query, w_key, w_value, math.gcd(bus_count, 256),
     )
     weights, attended, shifts = call(
-        weights_kernel, "weights", limit=56, first=0, count=pairs, scalars=scalars,
+        weights_kernel, "weights", limit=40, first=0, count=pairs, scalars=scalars,
         arrays=(queries, keys, values), out_first=0, dots=2, exps=1,
         outs=[
             bf16(pairs, bus_blocks, 3 * block_rows, 2 * block_rows),

time: 163 us -> 162 us (level)
  local copies, waits for them, and re-layouts: 8.78 us -> 13 us
  waiting for transfers between devices: 61.7 us -> 58.8 us
    unnamed x33 -> x39, local copies, waits for them, and re-layouts: 2.48 us -> 6.66 us
    all_to_all x2, waiting for transfers between devices: 35.9 us -> 32.7 us  [exchange(): return lax.all_to_all(value, 'bus', split_axis=0, concat_axis=0, tiled=True)]
where the time goes in v5:
time: 162 us; the launch traced here: 161 us
  Pallas kernels  69.1 us (43%)
  waiting for transfers between devices  58.8 us (36%)
  starting transfers between devices  17.7 us (11%)
  local copies, waits for them, and re-layouts  13 us (8%)
    pallas_call x4, Pallas kernels, by_pair(): pl.pallas_call(functools.partial(kernel, rows), grid_spec=pltpu.PrefetchS...  40 us
    all_to_all x2, waiting for transfers between devices, exchange(): return lax.all_to_all(value, 'bus', split_axis=0, concat_axis=0, tiled=True)  32.7 us
    ppermute x5, waiting for transfers between devices, swap(): return lax.ppermute(value, 'bus', [(i, i ^ bits) for i in range(devices)])  26.2 us
    pallas_call x1, Pallas kernels, encode(): pl.pallas_call(encode_kernel, grid_spec=pltpu.PrefetchScalarGridSpec(num_...  22.3 us
    all_to_all x2, starting transfers between devices, exchange(): return lax.all_to_all(value, 'bus', split_axis=0, concat_axis=0, tiled=True)  13.4 us
    unnamed x39, local copies, waits for them, and re-layouts  6.66 us
    pallas_call x1, Pallas kernels, settle(): pl.pallas_call(settle_kernel, grid_spec=pltpu.PrefetchScalarGridSpec(num_...  5.12 us
    ppermute x5, starting transfers between devices, swap(): return lax.ppermute(value, 'bus', [(i, i ^ bits) for i in range(devices)])  4.25 us
  transfers between devices with their start and end apart: 7, of which 5 were waited for; matrix products, arithmetic and copies ran while one was open for 6% of the time, Pallas kernels for 39%

profile of v5, /device:TPU:12, one launch (start us, length us, event | category | flops | bytes accessed | tf_op | source)
XLA Modules:
  0.0 161.1 jit_solution(12995758785188238450)
XLA Ops:
  0.6 0.0 copy-start.10
  0.6 0.0 copy-start.9
  0.7 0.0 copy-start.11
  0.7 6.4 %all-to-all-start = ((bf16[16,128,512]{2,1,0:T(8,128)(2,1)}), bf16[16,128,512]{2,1,0:T(8,128)(2,1)S(1)}, u32[]{:S(2)}, u32[]{:S(2)}) async-start(bf16[16,128,512]{2,1,0:T(8,128)(2,1)} %param.21), calls=%async_computation | async-start | bytes 4194304 | tf_op jit(solution)/shard_map/all_to_all | solution.py:389
  7.7 0.0 copy-done.10
  7.7 0.1 copy.19.neighbors_ref
  7.8 0.0 copy-done.9
  7.8 1.4 copy.18.order_ref
  9.2 0.0 copy-done.11
  9.2 22.3 %encode.1 = (bf16[2048,512]{1,0:T(8,128)(2,1)}, bf16[2048,512]{1,0:T(8,128)(2,1)}, bf16[2048,512]{1,0:T(8,128)(2,1)}) custom-call(s32[1]{0:T(128)S(6)} %copy.39.hour_ref, s32[2048,1]{1,0:T(8,128)} %copy.18.order_ref, bf16[2048,1024]{1,0:T(8,128)(2,1)} %bitcast.77, bf16[24,1024]{1,0:T(8,128)(2,1)} %table_ref.1, f32[1,1024]{1,0:T(1,128)} %bitcast.81, ...), custom_call_target="tpu_custom_call" | custom-call | flops 15032385536 | bytes 13631488 | tf_op jit(solution)/shard_map/encode/pallas_call | solution.py:55
  31.5 0.0 copy-start.1
  31.5 1.6 copy-done.1
  33.1 1.6 copy-done.3
  34.7 1.6 copy-done.5
  36.2 16.2 %weights.1 = (bf16[4,16,384,256]{3,2,1,0:T(8,128)(2,1)}, bf16[4,16,128,256]{3,2,1,0:T(8,128)(2,1)}, f32[4,16,256]{2,1,0:T(8,128)}) custom-call(s32[16,3]{1,0:T(8,128)S(1)} %copy.19.neighbors_ref, f32[8]{0:T(128)S(1)} %broadcast_multiply_fusion.scale_ref, bf16[2048,512]{1,0:T(8,128)(2,1)S(1)} %copy-done.1, bf16[2048,512]{1,0:T(8,128)(2,1)S(1)} %copy-done.3, ...), custom_call_target="tpu_custom_call" | custom-call | flops 1610612736 | bytes 100663296 | tf_op jit(solution)/shard_map/weights/pallas_call | solution.py:344
  52.5 1.8 %all-to-all-done = bf16[16,128,512]{2,1,0:T(8,128)(2,1)S(1)} async-done(((bf16[16,128,512]{2,1,0:T(8,128)(2,1)}), bf16[16,128,512]{2,1,0:T(8,128)(2,1)S(1)}, u32[]{:S(2)}, u32[]{:S(2)}) %all-to-all-start) | async-done | bytes 2097184 | tf_op jit(solution)/shard_map/all_to_all | solution.py:389
  54.3 4.8 %value_early.1 = (bf16[512,256]{1,0:T(8,128)(2,1)}, bf16[512,256]{1,0:T(8,128)(2,1)}, bf16[512,256]{1,0:T(8,128)(2,1)}, bf16[512,256]{1,0:T(8,128)(2,1)}) custom-call(s32[1]{0:T(128)} %bitcast.me_ref, bf16[4,16,384,256]{3,2,1,0:T(8,128)(2,1)} %get-tuple-element.21.w_ref, bf16[2048,512]{1,0:T(8,128)(2,1)S(1)} %bitcast.70), custom_call_target="tpu_custom_call" | custom-call | flops 402653184 | bytes 117440512 | tf_op jit(solution)/shard_map/value_early/pallas_call | solution.py:344
  59.1 0.1 collective-permute-start.2
  59.2 1.3 collective-permute-start.1
  60.5 2.1 %collective-permute-start = (bf16[4,128,256]{2,1,0:T(8,128)(2,1)}, bf16[4,128,256]{2,1,0:T(8,128)(2,1)}, u32[]{:S(2)}, u32[]{:S(2)}) collective-permute-start(bf16[4,128,256]{2,1,0:T(8,128)(2,1)} %bitcast.78), channel_id=1, source_target_pairs={{0,4},{1,5},{2,6},{3,7},{4,0},{5,1},{6,2},{7,3},{8,12},{9,13},{10,... | collective-permute-start | bytes 786440 | tf_op jit(solution)/shard_map/ppermute | solution.py:280
  62.6 4.9 %value_late.1.rest_0_ = bf16[2048,768]{1,0:T(8,128)(2,1)} custom-call(bf16[4,16,384,256]{3,2,1,0:T(8,128)(2,1)} %get-tuple-element.21.w_ref, bf16[2048,512]{1,0:T(8,128)(2,1)S(1)} %bitcast.71), custom_call_target="tpu_custom_call" | custom-call | flops 402653184 | bytes 117440512 | tf_op jit(solution)/shard_map/value_late/pallas_call | solution.py:344
  67.5 0.0 copy-done.2
  67.5 0.0 copy-done.4
  67.5 0.0 copy-done.6
  67.5 0.0 copy-done.7
  67.6 0.0 copy-done
  67.6 14.1 %key.1 = bf16[2048,768]{1,0:T(8,128)(2,1)} custom-call(s32[16,3]{1,0:T(8,128)S(1)} %copy.19.neighbors_ref, f32[8]{0:T(128)S(1)} %broadcast_multiply_fusion.scale_ref, bf16[2048,512]{1,0:T(8,128)(2,1)S(1)} %copy-done.2, bf16[2048,512]{1,0:T(8,128)(2,1)S(1)} %copy-done.4, bf16[2048,512]{1,0:T(8,128)(2,1)S(1)} %copy-done.6, ...), custom_call_target="tpu_custom_call", output_to_operand_aliasing={{}: (8, {})} | custom-call | flops 2415919104 | bytes 252182528 | tf_op jit(solution)/shard_map/key/pallas_call | solution.py:344
  81.6 0.0 collective-permute-done.2
  81.6 0.9 collective-permute-done.1
  82.6 0.0 collective-permute-done
  82.6 7.0 %all-to-all-start.1 = ((bf16[16,128,768]{2,1,0:T(8,128)(2,1)}), bf16[16,128,768]{2,1,0:T(8,128)(2,1)S(1)}, u32[]{:S(2)}, u32[]{:S(2)}) async-start(bf16[16,128,768]{2,1,0:T(8,128)(2,1)} %bitcast.73), calls=%async_computation.1 | async-start | bytes 6291456 | tf_op jit(solution)/shard_map/all_to_all | solution.py:389
  89.6 1.0 slice_bitcast_fusion.2
  90.6 0.9 slice_bitcast_fusion
  91.6 0.1 pad_maximum_fusion
  91.6 0.6 collective-permute-start.3
  92.3 1.5 slice.77
  93.7 1.5 slice.78
  95.2 0.0 copy-done.8
  95.2 0.9 maximum_bitcast_fusion
  96.1 23.3 %collective-permute-done.3 = bf16[4,2,128,256]{3,2,1,0:T(8,128)(2,1)S(1)} collective-permute-done((bf16[4,2,128,256]{3,2,1,0:T(8,128)(2,1)S(1)}, bf16[4,2,128,256]{3,2,1,0:T(8,128)(2,1)S(1)}, u32[]{:S(2)}, u32[]{:S(2)}) %collective-permute-start.3) | collective-permute-done | bytes 524320 | tf_op jit(solution)/shard_map/ppermute | solution.py:280
  119.5 0.1 pad_maximum_fusion.1
  119.6 0.1 collective-permute-start.4
  119.6 1.9 %collective-permute-done.4 = bf16[4,2,128,256]{3,2,1,0:T(8,128)(2,1)S(1)} collective-permute-done((bf16[4,2,128,256]{3,2,1,0:T(8,128)(2,1)S(1)}, bf16[4,2,128,256]{3,2,1,0:T(8,128)(2,1)S(1)}, u32[]{:S(2)}, u32[]{:S(2)}) %collective-permute-start.4) | collective-permute-done | bytes 524320 | tf_op jit(solution)/shard_map/ppermute | solution.py:280
  121.6 0.8 slice_dynamic-update-slice_fusion.2
  122.5 0.8 slice_dynamic-update-slice_fusion.1
  123.4 5.1 %settle.1._ = bf16[16,128,512]{2,1,0:T(8,128)(2,1)} custom-call(s32[1]{0:T(128)} %bitcast.me_ref, bf16[16,128,256]{2,1,0:T(8,128)(2,1)S(1)} %fusion.x_ref), custom_call_target="tpu_custom_call" | custom-call | bytes 2097152 | tf_op jit(solution)/shard_map/settle/pallas_call | solution.py:263
  128.5 30.9 %all-to-all-done.1.late_ref = bf16[16,128,768]{2,1,0:T(8,128)(2,1)S(1)} async-done(((bf16[16,128,768]{2,1,0:T(8,128)(2,1)}), bf16[16,128,768]{2,1,0:T(8,128)(2,1)S(1)}, u32[]{:S(2)}, u32[]{:S(2)}) %all-to-all-start.1) | async-done | bytes 3145760 | tf_op jit(solution)/shard_map/all_to_all | solution.py:389
  159.4 1.8 %part.1 = (bf16[16,128,512]{2,1,0:T(8,128)(2,1)}, bf16[16,128,512]{2,1,0:T(8,128)(2,1)}) custom-call(bf16[16,128,768]{2,1,0:T(8,128)(2,1)S(1)} %all-to-all-done.1.late_ref, bf16[16,128,512]{2,1,0:T(8,128)(2,1)} %settle.1._), custom_call_target="tpu_custom_call", output_to_operand_aliasing={{1}: (1, {})} | custom-call | bytes 6291456 | tf_op jit(solution)/shard_map/part/pallas_call | solution.py:310
  (25 shorter events, 0.1 us)
Async XLA Ops:
  0.6 7.1 %copy-start.10 = (s32[16,3]{0,1:T(4,128)S(1)}, s32[16,3]{0,1:T(4,128)}, u32[]{:S(2)}) copy-start(s32[16,3]{0,1:T(4,128)} %param.20) | copy-start | bytes 580
  0.6 7.2 %copy-start.9 = (s32[2048]{0:T(1024)S(1)}, s32[2048]{0:T(1024)}, u32[]{:S(2)}) copy-start(s32[2048]{0:T(1024)} %param.15) | copy-start | bytes 24580
  0.7 8.5 %copy-start.11 = (f32[8]{0:T(128)S(1)}, f32[8]{0:T(128)}, u32[]{:S(2)}) copy-start(f32[8]{0:T(128)} %param.19) | copy-start | bytes 100
  0.7 53.7 %all-to-all-start = ((bf16[16,128,512]{2,1,0:T(8,128)(2,1)}), bf16[16,128,512]{2,1,0:T(8,128)(2,1)S(1)}, u32[]{:S(2)}, u32[]{:S(2)}) async-start(bf16[16,128,512]{2,1,0:T(8,128)(2,1)} %param.21), calls=%async_computation | async-start | bytes 4194304 | tf_op jit(solution)/shard_map/all_to_all | solution.py:389
  31.5 1.6 copy-start.1
  33.1 1.6 copy-start.3
  34.7 1.6 copy-start.5
  59.1 22.6 %collective-permute-start.2 = (bf16[4,128,256]{2,1,0:T(8,128)(2,1)}, bf16[4,128,256]{2,1,0:T(8,128)(2,1)S(1)}, u32[]{:S(2)}, u32[]{:S(2)}) collective-permute-start(bf16[4,128,256]{2,1,0:T(8,128)(2,1)} %bitcast.80), channel_id=1, source_target_pairs={{0,12},{1,13},{2,14},{3,15},{4,8},{5,9},{6,10},{7,11},{8,4},{9,5},... | collective-permute-start | bytes 786440 | tf_op jit(solution)/shard_map/ppermute | solution.py:280
  59.2 23.4 %collective-permute-start.1 = (bf16[4,128,256]{2,1,0:T(8,128)(2,1)}, bf16[4,128,256]{2,1,0:T(8,128)(2,1)}, u32[]{:S(2)}, u32[]{:S(2)}) collective-permute-start(bf16[4,128,256]{2,1,0:T(8,128)(2,1)} %bitcast.79), channel_id=1, source_target_pairs={{0,8},{1,9},{2,10},{3,11},{4,12},{5,13},{6,14},{7,15},{8,0},{9,1},... | collective-permute-start | bytes 786440 | tf_op jit(solution)/shard_map/ppermute | solution.py:280
  60.5 7.0 %copy-start.2 = (bf16[2048,512]{1,0:T(8,128)(2,1)S(1)}, bf16[2048,512]{1,0:T(8,128)(2,1)}, u32[]{:S(2)}) copy-start(bf16[2048,512]{1,0:T(8,128)(2,1)} %get-tuple-element.18.q_ref) | copy-start | bytes 6291460
  60.5 7.0 %copy-start.4 = (bf16[2048,512]{1,0:T(8,128)(2,1)S(1)}, bf16[2048,512]{1,0:T(8,128)(2,1)}, u32[]{:S(2)}) copy-start(bf16[2048,512]{1,0:T(8,128)(2,1)} %get-tuple-element.19.k_ref) | copy-start | bytes 6291460
  60.5 7.0 %copy-start.6 = (bf16[2048,512]{1,0:T(8,128)(2,1)S(1)}, bf16[2048,512]{1,0:T(8,128)(2,1)}, u32[]{:S(2)}) copy-start(bf16[2048,512]{1,0:T(8,128)(2,1)} %get-tuple-element.20.v_ref) | copy-start | bytes 6291460
  60.5 7.0 %copy-start.7 = (f32[4,16,256]{2,1,0:T(8,128)S(1)}, f32[4,16,256]{2,1,0:T(8,128)}, u32[]{:S(2)}) copy-start(f32[4,16,256]{2,1,0:T(8,128)} %get-tuple-element.28.shift_ref) | copy-start | bytes 196612
  60.5 22.0 %collective-permute-start = (bf16[4,128,256]{2,1,0:T(8,128)(2,1)}, bf16[4,128,256]{2,1,0:T(8,128)(2,1)}, u32[]{:S(2)}, u32[]{:S(2)}) collective-permute-start(bf16[4,128,256]{2,1,0:T(8,128)(2,1)} %bitcast.78), channel_id=1, source_target_pairs={{0,4},{1,5},{2,6},{3,7},{4,0},{5,1},{6,2},{7,3},{8,12},{9,13},{10,... | collective-permute-start | bytes 786440 | tf_op jit(solution)/shard_map/ppermute | solution.py:280
  62.6 4.9 %copy-start = (bf16[4,16,128,256]{3,2,1,0:T(8,128)(2,1)S(1)}, bf16[4,16,128,256]{3,2,1,0:T(8,128)(2,1)}, u32[]{:S(2)}) copy-start(bf16[4,16,128,256]{3,2,1,0:T(8,128)(2,1)} %get-tuple-element.27.attended_ref) | copy-start | bytes 12582916
  82.6 76.8 %all-to-all-start.1 = ((bf16[16,128,768]{2,1,0:T(8,128)(2,1)}), bf16[16,128,768]{2,1,0:T(8,128)(2,1)S(1)}, u32[]{:S(2)}, u32[]{:S(2)}) async-start(bf16[16,128,768]{2,1,0:T(8,128)(2,1)} %bitcast.73), calls=%async_computation.1 | async-start | bytes 6291456 | tf_op jit(solution)/shard_map/all_to_all | solution.py:389
  89.6 5.6 %copy-start.8 = (bf16[512,256]{1,0:T(8,128)(2,1)S(1)}, bf16[512,256]{1,0:T(8,128)(2,1)}, u32[]{:S(2)}) copy-start(bf16[512,256]{1,0:T(8,128)(2,1)} %get-tuple-element.22) | copy-start | bytes 786436
  91.6 27.9 %collective-permute-start.3 = (bf16[4,2,128,256]{3,2,1,0:T(8,128)(2,1)S(1)}, bf16[4,2,128,256]{3,2,1,0:T(8,128)(2,1)S(1)}, u32[]{:S(2)}, u32[]{:S(2)}) collective-permute-start(bf16[4,2,128,256]{3,2,1,0:T(8,128)(2,1)S(1)} %pad_maximum_fusion), channel_id=1, source_target_pairs={{0,2},{1,3},{2,0},{3,1},{4,6},{5,7},{6,4},{7,5},{8,10},{9,11},{10,... | collective-permute-start | bytes 1572872 | tf_op jit(solution)/shard_map/ppermute | solution.py:280
  119.6 2.0 %collective-permute-start.4 = (bf16[4,2,128,256]{3,2,1,0:T(8,128)(2,1)S(1)}, bf16[4,2,128,256]{3,2,1,0:T(8,128)(2,1)S(1)}, u32[]{:S(2)}, u32[]{:S(2)}) collective-permute-start(bf16[4,2,128,256]{3,2,1,0:T(8,128)(2,1)S(1)} %pad_maximum_fusion.1), channel_id=1, source_target_pairs={{0,1},{1,0},{2,3},{3,2},{4,5},{5,4},{6,7},{7,6},{8,9},{9,8},{10,11... | collective-permute-start | bytes 1572872 | tf_op jit(solution)/shard_map/ppermute | solution.py:280
